TPU v7x, 32 devices: a whole 2x2x4 slice. The times are simulated.
32 devices in a mesh: groups: 2 (over y), blk: 4 (over z), tile: 2 (over x), pair: 2 (over core).
Axes of the slice: x: 2, y: 2, z: 4, core: 2. Of those that a mesh axis runs over, the one named last changes fastest.
Arguments:
- left_tokens: bfloat16 [4, 1536, 768], P(('groups', 'pair'), 'blk', 'tile'), parts along dimension 0, may hold values from -32 to 32
- right_tokens: bfloat16 [4, 1536, 768], P(('groups', 'pair'), 'blk', 'tile'), parts along dimension 0, may hold values from -32 to 32
- self_qkv: bfloat16 [3, 768, 512], P(None, None, 'tile'), may hold values from -1 to 1
- self_out: bfloat16 [512, 768], P('tile'), may hold values from -0.25 to 0.25
- cross_qkv: bfloat16 [3, 768, 512], P(None, None, 'tile'), may hold values from -1 to 1
- cross_out: bfloat16 [512, 768], P('tile'), may hold values from -0.25 to 0.25
- reassemble: bfloat16 [768, 256], P('tile'), may hold values from -0.21875 to 0.21875
- conv_weight: bfloat16 [3, 3, 256, 256], replicated, may hold values from -0.125 to 0.125
Outputs:
- joined: bfloat16 [4, 12, 128, 256], P(('groups', 'pair'), 'blk', 'tile'), parts along dimension 0
There are 2 independent parts, one for each index of `groups`. A program takes and returns all parts, laid end to end along the dimension named above; an argument that names none is the same for every part. Nothing has to cross between parts.
All inputs are finite; a program needn't handle non-finite values.
Results may differ from a plain program's by a relative error of at most 0.018.
Values may be sent and summed in bfloat16 or wider, within the bound.
A program may use at most 64 MiB of HBM per device.

v0:
```python
import jax
import jax.numpy as jnp
from jax import lax
from jax.sharding import PartitionSpec as P

HD = 64
CH = 256
GRID_W = 128


def padded_2(cells, sides, width):
    for axis, dim in sides:
        count = lax.axis_size(axis)
        ends = count - 1
        head = lax.slice_in_dim(cells, 0, width, axis=dim)
        tail = lax.slice_in_dim(cells, cells.shape[dim] - width, cells.shape[dim], axis=dim)
        cells = jnp.concatenate(
            [
                lax.ppermute(tail, axis, [(i, (i + 1) % count) for i in range(ends)]),
                cells,
                lax.ppermute(head, axis, [((i + 1) % count, i) for i in range(ends)]),
            ],
            axis=dim,
        )
    return cells


def layer_norm(values):
    widened = values.astype(jnp.float32)
    centred = widened - jnp.mean(widened, axis=-1, keepdims=True)
    variance = jnp.mean(centred * centred, axis=-1, keepdims=True)
    return (centred * lax.rsqrt(variance + 1e-06)).astype(jnp.bfloat16)


def project_rows(normed, weight):
    return jnp.dot(normed, weight, preferred_element_type=jnp.float32).astype(jnp.bfloat16)


def initial_state(queries):
    query_count = queries.shape[0]
    head_count = queries.shape[1] // HD
    return (
        jnp.full((head_count, query_count), -1e30, jnp.float32),
        jnp.zeros((head_count, query_count), jnp.float32),
        jnp.zeros(queries.shape, jnp.float32),
    )


def attend_keys(running, queries, keys_rows, values_rows):
    maxima, totals, accumulated = running
    query_count = queries.shape[0]
    head_count = queries.shape[1] // HD
    key_count = keys_rows.shape[0]
    scores = jnp.einsum(
        "qhd,khd->hqk",
        queries.reshape(query_count, head_count, HD),
        keys_rows.reshape(key_count, head_count, HD),
        preferred_element_type=jnp.float32,
    ) * HD ** (-0.5)
    new_maxima = jnp.maximum(maxima, jnp.max(scores, axis=2))
    correction = jnp.exp(maxima - new_maxima)
    expanded = jnp.exp(scores - new_maxima[:, :, None])
    totals = totals * correction + jnp.sum(expanded, axis=2)
    mixed = jnp.einsum(
        "hqk,khd->qhd",
        expanded.astype(jnp.bfloat16),
        values_rows.reshape(key_count, head_count, HD),
        preferred_element_type=jnp.float32,
    )
    accumulated = (
        accumulated.reshape(query_count, head_count, HD) * correction.T[:, :, None] + mixed
    )
    return (new_maxima, totals, accumulated.reshape(query_count, head_count * HD))


def fold_keys(running, queries, keys_rows, values_rows):
    key_count = keys_rows.shape[0]
    block_rows = max((divisor for divisor in range(1, 1025) if key_count % divisor == 0))
    if block_rows == key_count:
        return attend_keys(running, queries, keys_rows, values_rows)
    stacked_keys = keys_rows.reshape(key_count // block_rows, block_rows, keys_rows.shape[1])
    stacked_values = values_rows.reshape(key_count // block_rows, block_rows, values_rows.shape[1])

    def step_block(current, blocks):
        return (attend_keys(current, queries, blocks[0], blocks[1]), None)

    result, unused = lax.scan(step_block, running, (stacked_keys, stacked_values))
    return result


def finish_state(running):
    maxima, totals, accumulated = running
    query_count = accumulated.shape[0]
    head_count = accumulated.shape[1] // HD
    normalized = accumulated.reshape(query_count, head_count, HD) / totals.T[:, :, None]
    return normalized.reshape(query_count, head_count * HD).astype(jnp.bfloat16)


def body(
    left_tokens, right_tokens, self_qkv, self_out, cross_qkv, cross_out, reassemble, conv_weight
):
    left_full, right_full = (
        lax.all_gather(left_tokens, "tile", axis=2, tiled=True),
        lax.all_gather(right_tokens, "tile", axis=2, tiled=True),
    )
    left_rows = left_full[0]
    left_normed = layer_norm(left_rows)
    right_normed = layer_norm(right_full[0])
    self_query = project_rows(left_normed, self_qkv[0])
    self_key = project_rows(left_normed, self_qkv[1])
    self_value = project_rows(left_normed, self_qkv[2])
    cross_key = project_rows(right_normed, cross_qkv[1])
    cross_value = project_rows(right_normed, cross_qkv[2])
    pieces = (
        lax.all_gather(self_key, "blk", axis=0, tiled=True),
        lax.all_gather(self_value, "blk", axis=0, tiled=True),
    )
    self_state = fold_keys(initial_state(self_query), self_query, pieces[0], pieces[1])
    self_mixed = finish_state(self_state)
    self_term = jnp.dot(self_mixed, self_out, preferred_element_type=jnp.float32)
    self_share = lax.psum_scatter(
        self_term.astype(jnp.bfloat16), "tile", scatter_dimension=1, tiled=True
    ).astype(jnp.float32)
    updated = (left_tokens[0].astype(jnp.float32) + self_share).astype(jnp.bfloat16)
    updated_full = lax.all_gather(updated, "tile", axis=1, tiled=True)
    updated_normed = layer_norm(updated_full)
    cross_query = project_rows(updated_normed, cross_qkv[0])
    pieces = (
        lax.all_gather(cross_key, "blk", axis=0, tiled=True),
        lax.all_gather(cross_value, "blk", axis=0, tiled=True),
    )
    cross_state = fold_keys(initial_state(cross_query), cross_query, pieces[0], pieces[1])
    cross_mixed = finish_state(cross_state)
    cross_share = lax.psum_scatter(
        jnp.dot(cross_mixed, cross_out, preferred_element_type=jnp.float32).astype(jnp.bfloat16),
        "tile",
        scatter_dimension=1,
        tiled=True,
    ).astype(jnp.float32)
    final_tokens = (updated.astype(jnp.float32) + cross_share).astype(jnp.bfloat16)
    band_rows = final_tokens.shape[0] // GRID_W
    partial_map = jnp.dot(final_tokens, reassemble, preferred_element_type=jnp.float32).reshape(
        band_rows, GRID_W, CH
    )
    feature_map = lax.psum_scatter(
        partial_map.astype(jnp.bfloat16), "tile", scatter_dimension=1, tiled=True
    )
    column_count = feature_map.shape[1]
    activated = jnp.maximum(feature_map, jnp.zeros((), jnp.bfloat16))
    padded = padded_2(activated, (("blk", 0), ("tile", 1)), 1)
    stacked = jnp.concatenate(
        [
            padded[row_shift : row_shift + band_rows, col_shift : col_shift + column_count]
            for row_shift in range(3)
            for col_shift in range(3)
        ],
        axis=-1,
    )
    convolved = jnp.dot(
        stacked.reshape(band_rows * column_count, 9 * CH),
        conv_weight.reshape(9 * CH, CH),
        preferred_element_type=jnp.float32,
    )
    joined = (
        feature_map.astype(jnp.float32) + convolved.reshape(band_rows, column_count, CH)
    ).astype(jnp.bfloat16)
    return joined[None]


def solution(mesh):
    placed = (
        P(("groups", "pair"), "blk", "tile"),
        P(("groups", "pair"), "blk", "tile"),
        P(None, None, "tile"),
        P("tile", None),
        P(None, None, "tile"),
        P("tile", None),
        P("tile", None),
        P(),
    )
    return jax.shard_map(
        body,
        mesh=mesh,
        in_specs=placed,
        out_specs=P(("groups", "pair"), "blk", "tile", None),
        check_vma=False,
    )
```

profile of v0, /device:TPU:0, one launch (start us, length us, event | category | flops | bytes accessed | tf_op | source)
XLA Modules:
  0.0 217.8 jit_solution(9744858873867985740)
XLA Ops:
  6.5 11.0 %all_gather.21 = bf16[1,384,768]{2,1,0:T(8,128)(2,1)S(1)} all-gather(bf16[1,384,384]{2,1,0:T(8,128)(2,1)} %param.12), channel_id=1, replica_groups=mesh['groups'=2,'blk'=4,'tile'=2,'pair'=2] {'tile'}, dimensions={2}, use_global_device_ids=true | all-gather | bytes 884736 | tf_op jit(solution)/shard_map/all_gather | solution.py:103
  18.1 1.4 convolution_convert_fusion.8
  20.3 20.0 %all_gather.22 = bf16[1536,256]{1,0:T(8,128)(2,1)S(1)} all-gather(bf16[384,256]{1,0:T(8,128)(2,1)S(1)} %convolution_convert_fusion.8), channel_id=1, replica_groups=mesh['groups'=2,'blk'=4,'tile'=2,'pair'=2] {'blk'}, dimensions={0}, use_global_device_ids=true | all-gather | bytes 983040 | tf_op jit(solution)/shard_map/all_gather | solution.py:115
  40.3 18.1 %all_gather.23 = bf16[1536,256]{1,0:T(8,128)(2,1)} all-gather(bf16[384,256]{1,0:T(8,128)(2,1)S(1)} %convolution_convert_fusion.6), channel_id=1, replica_groups=mesh['groups'=2,'blk'=4,'tile'=2,'pair'=2] {'blk'}, dimensions={0}, use_global_device_ids=true | all-gather | bytes 983040 | tf_op jit(solution)/shard_map/all_gather | solution.py:116
  58.4 0.8 copy.20
  59.3 19.8 %while.30 = (s32[]{:T(128)}, f32[4,384]{1,0:T(4,128)S(1)}, f32[4,384]{1,0:T(4,128)S(1)}, f32[384,256]{0,1:T(8,128)S(1)}, bf16[2,768,256]{2,1,0:T(8,128)(2,1)S(1)...) while((s32[]{:T(128)}, f32[4,384]{1,0:T(4,128)S(1)}, ...), condition=%wide.region_5.0_spmd.clone, body=%wide.region_2.5_spmd.clone.sunk | while | flops 311632896 | bytes 38043784 | solution.py:87
  59.3 1.1 constant_dynamic-slice_fusion.6
  60.5 3.9 %bitcast_reduce_fusion.4 = (f32[4,384]{1,0:T(4,128)S(1)}, f32[4,768,384]{2,1,0:T(8,128)}) fusion(bf16[768,4,64]{0,2,1:T(8,128)(2,1)S(1)} %bitcast.186, bf16[384,4,64]{0,2,1:T(8,128)(2,1)} %bitcast.199), kind=kOutput, calls=%fused_computation.1.clone.1 | convolution fusion | flops 153352704 | bytes 5314560 | tf_op jit(solution)/shard_map/while/body/eval_jaxpr/qhd,khd->hqk/dot_general | solution.py:54
  64.6 3.5 %fusion.112 = f32[384,4,64]{0,2,1:T(8,128)S(1)} fusion(bf16[768,4,64]{0,2,1:T(8,128)(2,1)S(1)} %bitcast.187, f32[4,768,384]{2,1,0:T(8,128)} %get-tuple-element.301, f32[4,384]{1,0:T(4,128)S(1)} %get-tuple-element.336, f32[384,4,64]{0,2,1:T(8,128)S(1)} %bitcast.192, f32[384,4]{0,1:T(4,128)S(1)} %get-tuple-element.303), kind=kOutput, calls=%fused_computation.9.clone.1 | convolution fusion | flops 154730496 | bytes 5910528 | tf_op jit(solution)/shard_map/while/body/eval_jaxpr/hqk,khd->qhd/dot_general | solution.py:64
  68.3 0.8 fusion.110
  69.2 1.1 constant_dynamic-slice_fusion.6
  70.4 3.9 %bitcast_reduce_fusion.4 = (f32[4,384]{1,0:T(4,128)S(1)}, f32[4,768,384]{2,1,0:T(8,128)}) fusion(bf16[768,4,64]{0,2,1:T(8,128)(2,1)S(1)} %bitcast.186, bf16[384,4,64]{0,2,1:T(8,128)(2,1)} %bitcast.199), kind=kOutput, calls=%fused_computation.1.clone.1 | convolution fusion | flops 153352704 | bytes 5314560 | tf_op jit(solution)/shard_map/while/body/eval_jaxpr/qhd,khd->hqk/dot_general | solution.py:54
  74.5 3.5 %fusion.112 = f32[384,4,64]{0,2,1:T(8,128)S(1)} fusion(bf16[768,4,64]{0,2,1:T(8,128)(2,1)S(1)} %bitcast.187, f32[4,768,384]{2,1,0:T(8,128)} %get-tuple-element.301, f32[4,384]{1,0:T(4,128)S(1)} %get-tuple-element.336, f32[384,4,64]{0,2,1:T(8,128)S(1)} %bitcast.192, f32[384,4]{0,1:T(4,128)S(1)} %get-tuple-element.303), kind=kOutput, calls=%fused_computation.9.clone.1 | convolution fusion | flops 154730496 | bytes 5910528 | tf_op jit(solution)/shard_map/while/body/eval_jaxpr/hqk,khd->qhd/dot_general | solution.py:64
  78.2 0.8 fusion.110
  79.1 1.4 convolution_convert_fusion.1
  80.5 1.0 copy.27
  81.6 9.7 %all_gather.24 = bf16[1,384,768]{2,1,0:T(8,128)(2,1)S(1)} all-gather(bf16[1,384,384]{2,1,0:T(8,128)(2,1)S(1)} %copy-done.7), channel_id=1, replica_groups=mesh['groups'=2,'blk'=4,'tile'=2,'pair'=2] {'tile'}, dimensions={2}, use_global_device_ids=true | all-gather | bytes 884736 | tf_op jit(solution)/shard_map/all_gather | solution.py:104
  91.8 1.4 convolution_convert_fusion.3
  93.2 1.4 convolution_convert_fusion.5
  94.6 17.3 %all_gather.27 = bf16[1536,256]{1,0:T(8,128)(2,1)S(1)} all-gather(bf16[384,256]{1,0:T(8,128)(2,1)S(1)} %convolution_convert_fusion.3), channel_id=1, replica_groups=mesh['groups'=2,'blk'=4,'tile'=2,'pair'=2] {'blk'}, dimensions={0}, use_global_device_ids=true | all-gather | bytes 983040 | tf_op jit(solution)/shard_map/all_gather | solution.py:130
  111.9 16.3 %all_gather.25 = bf16[1536,256]{1,0:T(8,128)(2,1)} all-gather(bf16[384,256]{1,0:T(8,128)(2,1)S(1)} %convolution_convert_fusion.5), channel_id=1, replica_groups=mesh['groups'=2,'blk'=4,'tile'=2,'pair'=2] {'blk'}, dimensions={0}, use_global_device_ids=true | all-gather | bytes 983040 | tf_op jit(solution)/shard_map/all_gather | solution.py:129
  128.2 1.2 copy.28
  130.2 8.4 %all_gather.26 = bf16[384,768]{1,0:T(8,128)(2,1)S(1)} all-gather(bf16[384,384]{1,0:T(8,128)(2,1)S(1)} %fusion.51), channel_id=1, replica_groups=mesh['groups'=2,'blk'=4,'tile'=2,'pair'=2] {'tile'}, dimensions={1}, use_global_device_ids=true | all-gather | bytes 884736 | tf_op jit(solution)/shard_map/all_gather | solution.py:125
  139.1 1.4 convolution_convert_fusion.4
  140.4 0.8 copy.23
  141.3 19.8 %while.31 = (s32[]{:T(128)}, f32[4,384]{1,0:T(4,128)S(1)}, f32[4,384]{1,0:T(4,128)S(1)}, f32[384,256]{0,1:T(8,128)S(1)}, bf16[2,768,256]{2,1,0:T(8,128)(2,1)}, /...) while((s32[]{:T(128)}, f32[4,384]{1,0:T(4,128)S(1)}, ...), condition=%wide.region_14.15_spmd.clone, body=%wide.region_11.14_spmd.clone.sunk | while | flops 311632896 | bytes 38043784 | solution.py:87
  141.3 1.1 constant_dynamic-slice_fusion.7
  142.6 3.9 %bitcast_reduce_fusion.5 = (f32[4,384]{1,0:T(4,128)S(1)}, f32[4,768,384]{2,1,0:T(8,128)}) fusion(bf16[768,4,64]{0,2,1:T(8,128)(2,1)S(1)} %bitcast.188, bf16[384,4,64]{0,2,1:T(8,128)(2,1)} %bitcast.198), kind=kOutput, calls=%fused_computation.19.clone.1 | convolution fusion | flops 153352704 | bytes 5314560 | tf_op jit(solution)/shard_map/while/body/eval_jaxpr/qhd,khd->hqk/dot_general | solution.py:54
  146.6 3.5 %fusion.120 = f32[384,4,64]{0,2,1:T(8,128)S(1)} fusion(bf16[768,4,64]{0,2,1:T(8,128)(2,1)S(1)} %bitcast.189, f32[4,768,384]{2,1,0:T(8,128)} %get-tuple-element.314, f32[4,384]{1,0:T(4,128)S(1)} %get-tuple-element.363, f32[384,4,64]{0,2,1:T(8,128)S(1)} %bitcast.190, f32[384,4]{0,1:T(4,128)S(1)} %get-tuple-element.316), kind=kOutput, calls=%fused_computation.27.clone.1 | convolution fusion | flops 154730496 | bytes 5910528 | tf_op jit(solution)/shard_map/while/body/eval_jaxpr/hqk,khd->qhd/dot_general | solution.py:64
  150.4 0.8 fusion.118
  151.2 1.1 constant_dynamic-slice_fusion.7
  152.4 3.9 %bitcast_reduce_fusion.5 = (f32[4,384]{1,0:T(4,128)S(1)}, f32[4,768,384]{2,1,0:T(8,128)}) fusion(bf16[768,4,64]{0,2,1:T(8,128)(2,1)S(1)} %bitcast.188, bf16[384,4,64]{0,2,1:T(8,128)(2,1)} %bitcast.198), kind=kOutput, calls=%fused_computation.19.clone.1 | convolution fusion | flops 153352704 | bytes 5314560 | tf_op jit(solution)/shard_map/while/body/eval_jaxpr/qhd,khd->hqk/dot_general | solution.py:54
  156.5 3.5 %fusion.120 = f32[384,4,64]{0,2,1:T(8,128)S(1)} fusion(bf16[768,4,64]{0,2,1:T(8,128)(2,1)S(1)} %bitcast.189, f32[4,768,384]{2,1,0:T(8,128)} %get-tuple-element.314, f32[4,384]{1,0:T(4,128)S(1)} %get-tuple-element.363, f32[384,4,64]{0,2,1:T(8,128)S(1)} %bitcast.190, f32[384,4]{0,1:T(4,128)S(1)} %get-tuple-element.316), kind=kOutput, calls=%fused_computation.27.clone.1 | convolution fusion | flops 154730496 | bytes 5910528 | tf_op jit(solution)/shard_map/while/body/eval_jaxpr/hqk,khd->qhd/dot_general | solution.py:64
  160.3 0.8 fusion.118
  161.1 1.4 convolution_convert_fusion
  162.5 1.0 copy.29
  163.7 14.7 %reduce-scatter.12.cloned.1.call-done = bf16[384,384]{1,0:T(8,128)(2,1)} async-done(((bf16[768,384]{1,0:T(8,128)(2,1)}), bf16[384,384]{1,0:T(8,128)(2,1)}) %reduce-scatter.12.cloned.1.call-update) | async-done | bytes 294928
  178.4 1.2 copy.30
  179.6 0.9 convolution_convert_fusion.2
  180.5 11.2 %reduce-scatter.8.cloned.1.call-done = bf16[3,64,256]{2,1,0:T(8,128)(2,1)} async-done(((bf16[3,128,256]{2,1,0:T(8,128)(2,1)}), bf16[3,64,256]{2,1,0:T(8,128)(2,1)}) %reduce-scatter.8.cloned.1.call-update) | async-done | bytes 98320 | tf_op jit(solution)/shard_map/reduce_scatter | solution.py:145
  191.7 1.0 broadcast_maximum_fusion
  192.7 3.4 %collective-permute-start = (bf16[1,64,256]{2,1,0:T(8,128)(2,1)S(1)}, bf16[1,64,256]{2,1,0:T(8,128)(2,1)S(1)}, u32[]{:S(2)}, u32[]{:S(2)}) collective-permute-start(bf16[1,64,256]{2,1,0:T(8,128)(2,1)S(1)} %get-tuple-element.205), channel_id=1, source_target_pairs={{0,4},{4,8},{8,12},{1,5},{5,9},{9,13},{2,6},{6,10},{10,14},{3,7},{... | collective-permute-start | bytes 98312 | tf_op jit(solution)/shard_map/ppermute | solution.py:19
  196.1 1.3 collective-permute-start.1
  197.7 4.2 %collective-permute-done.1 = bf16[1,64,256]{2,1,0:T(8,128)(2,1)S(1)} collective-permute-done((bf16[1,64,256]{2,1,0:T(8,128)(2,1)S(1)}, bf16[1,64,256]{2,1,0:T(8,128)(2,1)S(1)}, u32[]{:S(2)}, u32[]{:S(2)}) %collective-permute-start.1) | collective-permute-done | bytes 32800 | tf_op jit(solution)/shard_map/ppermute | solution.py:21
  201.9 2.5 %collective-permute-start.2 = (bf16[5,1,256]{2,1,0:T(2,128)(2,1)S(1)}, bf16[5,1,256]{2,1,0:T(2,128)(2,1)S(1)}, u32[]{:S(2)}, u32[]{:S(2)}) collective-permute-start(bf16[5,1,256]{2,1,0:T(2,128)(2,1)S(1)} %get-tuple-element.204), channel_id=1, source_target_pairs={{0,2},{1,3},{4,6},{5,7},{8,10},{9,11},{12,14},{13,15},{16,18},{17,... | collective-permute-start | bytes 7688 | tf_op jit(solution)/shard_map/ppermute | solution.py:19
  204.4 1.3 collective-permute-start.3
  205.7 4.2 %collective-permute-done.3 = bf16[5,1,256]{2,1,0:T(2,128)(2,1)S(1)} collective-permute-done((bf16[5,1,256]{2,1,0:T(2,128)(2,1)S(1)}, bf16[5,1,256]{2,1,0:T(2,128)(2,1)S(1)}, u32[]{:S(2)}, u32[]{:S(2)}) %collective-permute-start.3) | collective-permute-done | bytes 2592 | tf_op jit(solution)/shard_map/ppermute | solution.py:21
  210.2 1.1 fusion.47
  (88 shorter events, 6.3 us)
Async XLA Ops:
  6.5 203.7 %copy-start = (bf16[3,3,256,256]{3,2,1,0:T(8,128)(2,1)S(1)}, bf16[3,3,256,256]{3,2,1,0:T(8,128)(2,1)}, u32[]{:S(2)}) copy-start(bf16[3,3,256,256]{3,2,1,0:T(8,128)(2,1)} %param.19) | copy-start | bytes 3538948
  6.5 121.6 %reduce-scatter.10.cloned.1.call-start = ((), (), s32[]{:S(2)}) async-start(), calls=%async_computation.4 | async-start | bytes 884736
  17.7 1.8 copy-start.9
  64.6 3.8 %copy-start.1 = (f32[4,768,384]{2,1,0:T(8,128)S(1)}, f32[4,768,384]{2,1,0:T(8,128)}, u32[]{:S(2)}) copy-start(f32[4,768,384]{2,1,0:T(8,128)} %get-tuple-element.301) | copy-start | bytes 14155780 | tf_op jit(solution)/shard_map/while
  74.5 3.8 %copy-start.1 = (f32[4,768,384]{2,1,0:T(8,128)S(1)}, f32[4,768,384]{2,1,0:T(8,128)}, u32[]{:S(2)}) copy-start(f32[4,768,384]{2,1,0:T(8,128)} %get-tuple-element.301) | copy-start | bytes 14155780 | tf_op jit(solution)/shard_map/while
  80.5 1.1 copy-start.7
  81.6 96.8 %reduce-scatter.12.cloned.1.call-start = ((), (), s32[]{:S(2)}) async-start(), calls=%async_computation.5 | async-start | bytes 884736
  94.6 34.8 %copy-start.5 = (bf16[1,384,384]{2,1,0:T(8,128)(2,1)S(1)}, bf16[1,384,384]{2,1,0:T(8,128)(2,1)}, u32[]{:S(2)}) copy-start(bf16[1,384,384]{2,1,0:T(8,128)(2,1)} %param.12) | copy-start | bytes 884740
  129.5 0.7 copy-start.3
  146.6 3.8 %copy-start.2 = (f32[4,768,384]{2,1,0:T(8,128)S(1)}, f32[4,768,384]{2,1,0:T(8,128)}, u32[]{:S(2)}) copy-start(f32[4,768,384]{2,1,0:T(8,128)} %get-tuple-element.314) | copy-start | bytes 14155780 | tf_op jit(solution)/shard_map/while
  156.5 3.8 %copy-start.2 = (f32[4,768,384]{2,1,0:T(8,128)S(1)}, f32[4,768,384]{2,1,0:T(8,128)}, u32[]{:S(2)}) copy-start(f32[4,768,384]{2,1,0:T(8,128)} %get-tuple-element.314) | copy-start | bytes 14155780 | tf_op jit(solution)/shard_map/while
  162.5 17.0 %copy-start.4 = (bf16[384,384]{1,0:T(8,128)(2,1)S(1)}, bf16[384,384]{1,0:T(8,128)(2,1)}, u32[]{:S(2)}) copy-start(bf16[384,384]{1,0:T(8,128)(2,1)} %copy-done.3) | copy-start | bytes 884740
  162.5 17.0 %copy-start.8 = (bf16[384,256]{1,0:T(8,128)(2,1)S(1)}, bf16[384,256]{1,0:T(8,128)(2,1)}, u32[]{:S(2)}) copy-start(bf16[384,256]{1,0:T(8,128)(2,1)} %param.18) | copy-start | bytes 589828
  163.6 28.1 %reduce-scatter.8.cloned.1.call-start = ((), (), s32[]{:S(2)}) async-start(), calls=%async_computation.3 | async-start | bytes 294912 | tf_op jit(solution)/shard_map/reduce_scatter | solution.py:145
  191.7 18.3 %copy-start.6 = (bf16[3,64,256]{2,1,0:T(8,128)(2,1)S(1)}, bf16[3,64,256]{2,1,0:T(8,128)(2,1)}, u32[]{:S(2)}) copy-start(bf16[3,64,256]{2,1,0:T(8,128)(2,1)} %reduce-scatter.8.cloned.1.call-done) | copy-start | bytes 294916
  192.7 5.0 %collective-permute-start = (bf16[1,64,256]{2,1,0:T(8,128)(2,1)S(1)}, bf16[1,64,256]{2,1,0:T(8,128)(2,1)S(1)}, u32[]{:S(2)}, u32[]{:S(2)}) collective-permute-start(bf16[1,64,256]{2,1,0:T(8,128)(2,1)S(1)} %get-tuple-element.205), channel_id=1, source_target_pairs={{0,4},{4,8},{8,12},{1,5},{5,9},{9,13},{2,6},{6,10},{10,14},{3,7},{... | collective-permute-start | bytes 98312 | tf_op jit(solution)/shard_map/ppermute | solution.py:19
  196.1 5.8 %collective-permute-start.1 = (bf16[1,64,256]{2,1,0:T(8,128)(2,1)S(1)}, bf16[1,64,256]{2,1,0:T(8,128)(2,1)S(1)}, u32[]{:S(2)}, u32[]{:S(2)}) collective-permute-start(bf16[1,64,256]{2,1,0:T(8,128)(2,1)S(1)} %get-tuple-element.206), channel_id=1, source_target_pairs={{4,0},{8,4},{12,8},{5,1},{9,5},{13,9},{6,2},{10,6},{14,10},{7,3},{... | collective-permute-start | bytes 98312 | tf_op jit(solution)/shard_map/ppermute | solution.py:21
  201.9 3.8 %collective-permute-start.2 = (bf16[5,1,256]{2,1,0:T(2,128)(2,1)S(1)}, bf16[5,1,256]{2,1,0:T(2,128)(2,1)S(1)}, u32[]{:S(2)}, u32[]{:S(2)}) collective-permute-start(bf16[5,1,256]{2,1,0:T(2,128)(2,1)S(1)} %get-tuple-element.204), channel_id=1, source_target_pairs={{0,2},{1,3},{4,6},{5,7},{8,10},{9,11},{12,14},{13,15},{16,18},{17,... | collective-permute-start | bytes 7688 | tf_op jit(solution)/shard_map/ppermute | solution.py:19
  204.4 5.5 %collective-permute-start.3 = (bf16[5,1,256]{2,1,0:T(2,128)(2,1)S(1)}, bf16[5,1,256]{2,1,0:T(2,128)(2,1)S(1)}, u32[]{:S(2)}, u32[]{:S(2)}) collective-permute-start(bf16[5,1,256]{2,1,0:T(2,128)(2,1)S(1)} %get-tuple-element.203), channel_id=1, source_target_pairs={{2,0},{3,1},{6,4},{7,5},{10,8},{11,9},{14,12},{15,13},{18,16},{19,... | collective-permute-start | bytes 7688 | tf_op jit(solution)/shard_map/ppermute | solution.py:21
Sparse Core Ops, SparseCore 0:
  81.7 14.7 reduce-scatter.9
  163.7 14.6 reduce-scatter.11
  180.7 11.0 reduce-scatter.7
where the time goes:
time: 219 us; the launch traced here: 218 us
  blocking collectives  101 us (46%)
  matrix products  40.5 us (18%)
  waiting for transfers between devices  34.7 us (16%)
  local copies, waits for them, and re-layouts  13.6 us (6%)
  between operations  13.5 us (6%)
  starting transfers between devices  8.52 us (4%)
  other arithmetic  5.96 us (3%)
    all_gather x1, blocking collectives, body(): lax.all_gather(self_key, 'blk', axis=0, tiled=True)  20 us
    all_gather x1, blocking collectives, body(): lax.all_gather(self_value, 'blk', axis=0, tiled=True)  18.1 us
    all_gather x1, blocking collectives, body(): lax.all_gather(cross_value, 'blk', axis=0, tiled=True)  17.3 us
    all_gather x1, blocking collectives, body(): lax.all_gather(cross_key, 'blk', axis=0, tiled=True)  16.3 us
    dot_general x4, matrix products, attend_keys(): jnp.einsum('qhd,khd->hqk', queries.reshape(query_count, head_count, HD),...  15.5 us
    unnamed x5, waiting for transfers between devices  14.8 us
    dot_general x4, matrix products, attend_keys(): jnp.einsum('hqk,khd->qhd', expanded.astype(jnp.bfloat16), values_rows.res...  14 us
    reduce_scatter x1, waiting for transfers between devices, body(): lax.psum_scatter(partial_map.astype(jnp.bfloat16), 'tile', scatter_dimens...  11.2 us
  transfers between devices with their start and end apart: 7, of which 5 were waited for; matrix products, arithmetic and copies ran while one was open for 1% of the time, Pallas kernels for 0%

commit v1 on v0

--- a/solution.py
+++ b/solution.py
@@ -99,55 +99,64 @@
 def body(
     left_tokens, right_tokens, self_qkv, self_out, cross_qkv, cross_out, reassemble, conv_weight
 ):
-    left_full, right_full = (
-        lax.all_gather(left_tokens, "tile", axis=2, tiled=True),
-        lax.all_gather(right_tokens, "tile", axis=2, tiled=True),
+    tiles = lax.axis_size("tile")
+    tile_index = lax.axis_index("tile")
+    token_count, feature_share = left_tokens.shape[1], left_tokens.shape[2]
+    packed = jnp.concatenate(
+        [left_tokens[0].reshape(-1), right_tokens[0].reshape(-1), reassemble.reshape(-1)]
     )
-    left_rows = left_full[0]
-    left_normed = layer_norm(left_rows)
-    right_normed = layer_norm(right_full[0])
+    gathered = lax.all_gather(packed, "tile", axis=0)
+    block = token_count * feature_share
+
+    def features(offset):
+        return jnp.concatenate(
+            [gathered[i, offset : offset + block].reshape(token_count, feature_share) for i in range(tiles)],
+            axis=1,
+        )
+
+    left_full = features(0)
+    right_full = features(block)
+    reassemble_full = gathered[:, 2 * block :].reshape(tiles * reassemble.shape[0], CH)
+    left_normed = layer_norm(left_full)
+    right_normed = layer_norm(right_full)
     self_query = project_rows(left_normed, self_qkv[0])
-    self_key = project_rows(left_normed, self_qkv[1])
-    self_value = project_rows(left_normed, self_qkv[2])
-    cross_key = project_rows(right_normed, cross_qkv[1])
-    cross_value = project_rows(right_normed, cross_qkv[2])
-    pieces = (
-        lax.all_gather(self_key, "blk", axis=0, tiled=True),
-        lax.all_gather(self_value, "blk", axis=0, tiled=True),
+    projected = jnp.stack(
+        [
+            project_rows(left_normed, self_qkv[1]),
+            project_rows(left_normed, self_qkv[2]),
+            project_rows(right_normed, cross_qkv[1]),
+            project_rows(right_normed, cross_qkv[2]),
+        ]
     )
+    pieces = lax.all_gather(projected, "blk", axis=1, tiled=True)
     self_state = fold_keys(initial_state(self_query), self_query, pieces[0], pieces[1])
     self_mixed = finish_state(self_state)
     self_term = jnp.dot(self_mixed, self_out, preferred_element_type=jnp.float32)
-    self_share = lax.psum_scatter(
-        self_term.astype(jnp.bfloat16), "tile", scatter_dimension=1, tiled=True
-    ).astype(jnp.float32)
-    updated = (left_tokens[0].astype(jnp.float32) + self_share).astype(jnp.bfloat16)
-    updated_full = lax.all_gather(updated, "tile", axis=1, tiled=True)
-    updated_normed = layer_norm(updated_full)
+    self_sum = lax.psum(self_term.astype(jnp.bfloat16), "tile").astype(jnp.float32)
+    updated = (left_full.astype(jnp.float32) + self_sum).astype(jnp.bfloat16)
+    updated_normed = layer_norm(updated)
     cross_query = project_rows(updated_normed, cross_qkv[0])
-    pieces = (
-        lax.all_gather(cross_key, "blk", axis=0, tiled=True),
-        lax.all_gather(cross_value, "blk", axis=0, tiled=True),
+    cross_state = fold_keys(initial_state(cross_query), cross_query, pieces[2], pieces[3])
+    cross_mixed = finish_state(cross_state)
+    cross_term = jnp.dot(cross_mixed, cross_out, preferred_element_type=jnp.float32)
+    cross_sum = lax.psum(cross_term.astype(jnp.bfloat16), "tile").astype(jnp.float32)
+    final_tokens = (updated.astype(jnp.float32) + cross_sum).astype(jnp.bfloat16)
+    band_rows = token_count // GRID_W
+    column_count = GRID_W // tiles
+    grid = jnp.pad(final_tokens.reshape(band_rows, GRID_W, -1), ((0, 0), (1, 1), (0, 0)))
+    window = lax.dynamic_slice_in_dim(grid, tile_index * column_count, column_count + 2, axis=1)
+    wide_map = (
+        jnp.dot(
+            window.reshape(band_rows * (column_count + 2), -1),
+            reassemble_full,
+            preferred_element_type=jnp.float32,
+        )
+        .astype(jnp.bfloat16)
+        .reshape(band_rows, column_count + 2, CH)
     )
-    cross_state = fold_keys(initial_state(cross_query), cross_query, pieces[0], pieces[1])
-    cross_mixed = finish_state(cross_state)
-    cross_share = lax.psum_scatter(
-        jnp.dot(cross_mixed, cross_out, preferred_element_type=jnp.float32).astype(jnp.bfloat16),
-        "tile",
-        scatter_dimension=1,
-        tiled=True,
-    ).astype(jnp.float32)
-    final_tokens = (updated.astype(jnp.float32) + cross_share).astype(jnp.bfloat16)
-    band_rows = final_tokens.shape[0] // GRID_W
-    partial_map = jnp.dot(final_tokens, reassemble, preferred_element_type=jnp.float32).reshape(
-        band_rows, GRID_W, CH
-    )
-    feature_map = lax.psum_scatter(
-        partial_map.astype(jnp.bfloat16), "tile", scatter_dimension=1, tiled=True
-    )
-    column_count = feature_map.shape[1]
-    activated = jnp.maximum(feature_map, jnp.zeros((), jnp.bfloat16))
-    padded = padded_2(activated, (("blk", 0), ("tile", 1)), 1)
+    feature_map = wide_map[:, 1 : column_count + 1]
+    activated = jnp.maximum(wide_map, jnp.zeros((), jnp.bfloat16))
+    padded = padded_2(activated, (("blk", 0),), 1)
     stacked = jnp.concatenate(
         [
             padded[row_shift : row_shift + band_rows, col_shift : col_shift + column_count]

time: 219 us -> 235 us (1.073)
  waiting for transfers between devices: 34.7 us -> 155 us
  blocking collectives: 101 us -> 0 us
  matrix products: 40.5 us -> 23 us
  local copies, waits for them, and re-layouts: 13.6 us -> 27.7 us
  starting transfers between devices: 8.52 us -> 4.99 us
  other arithmetic: 5.96 us -> 9.46 us
    all_gather x7 -> x0, blocking collectives: 101 us -> none  [the longest x1 20 us: body(): lax.all_gather(self_key, 'blk', axis=0, tiled=True)]
    all_gather x0 -> x2, waiting for transfers between devices: none -> 92 us  [the longest x1 62 us: body(): pieces = lax.all_gather(projected, 'blk', axis=1, tiled=True)]
    psum x0 -> x2, waiting for transfers between devices: none -> 58.6 us  [the longest x1 30 us: body(): lax.psum(cross_term.astype(jnp.bfloat16), 'tile').astype(jnp.float32)]
    unnamed x5 -> x4, waiting for transfers between devices: 14.8 us -> 0.07 us
    reduce_scatter x1 -> x0, waiting for transfers between devices: 11.2 us -> none  [body(): lax.psum_scatter(partial_map.astype(jnp.bfloat16), 'tile', scatter_dimens...]
    slice x1 -> x5, local copies, waits for them, and re-layouts: 0.01 us -> 10.5 us  [the longest x1 7.18 us: features(): gathered[i, offset:offset + block].reshape(token_count, feature_share)]
    dot_general x4, matrix products: 14 us -> 4.05 us  [attend_keys(): jnp.einsum('hqk,khd->qhd', expanded.astype(jnp.bfloat16), values_rows.res...]
    dot_general x4, matrix products: 15.5 us -> 7.05 us  [attend_keys(): jnp.einsum('qhd,khd->hqk', queries.reshape(query_count, head_count, HD),...]
  transfers between devices with their start and end apart: 7 -> 6, of which waited for: 5 -> 6; matrix products, arithmetic and copies ran while one was open for 1% -> 1% of each run, Pallas kernels for 0% -> 0%
where the time goes in v1:
time: 235 us; the launch traced here: 234 us
  waiting for transfers between devices  155 us (66%)
  local copies, waits for them, and re-layouts  27.7 us (12%)
  matrix products  23 us (10%)
  between operations  13.5 us (6%)
  other arithmetic  9.46 us (4%)
  starting transfers between devices  4.99 us (2%)
    all_gather x1, waiting for transfers between devices, body(): pieces = lax.all_gather(projected, 'blk', axis=1, tiled=True)  62 us
    all_gather x1, waiting for transfers between devices, body(): gathered = lax.all_gather(packed, 'tile', axis=0)  30 us
    psum x1, waiting for transfers between devices, body(): lax.psum(cross_term.astype(jnp.bfloat16), 'tile').astype(jnp.float32)  30 us
    psum x1, waiting for transfers between devices, body(): lax.psum(self_term.astype(jnp.bfloat16), 'tile').astype(jnp.float32)  28.6 us
    slice x1, local copies, waits for them, and re-layouts, features(): gathered[i, offset:offset + block].reshape(token_count, feature_share)  7.18 us
    dot_general x4, matrix products, attend_keys(): jnp.einsum('qhd,khd->hqk', queries.reshape(query_count, head_count, HD),...  7.05 us
    dot_general x6, matrix products, project_rows(): jnp.dot(normed, weight, preferred_element_type=jnp.float32)  6.08 us
    dynamic_slice x12, local copies, waits for them, and re-layouts, fold_keys(): lax.scan(step_block, running, (stacked_keys, stacked_values))  5.79 us
  transfers between devices with their start and end apart: 6, of which 6 were waited for; matrix products, arithmetic and copies ran while one was open for 1% of the time, Pallas kernels for 0%

profile of v1, /device:TPU:0, one launch (start us, length us, event | category | flops | bytes accessed | tf_op | source)
XLA Modules:
  0.0 234.0 jit_solution(1149109852763883605)
XLA Ops:
  6.5 1.2 copy.31
  7.7 1.1 reshape_squeeze.30
  9.0 0.9 pad_maximum_fusion
  10.0 30.0 %all-gather.6.cloned.1.call-done = bf16[786432]{0:T(1024)(128)(2,1)} async-done(((bf16[393216]{0:T(1024)(128)(2,1)}), bf16[786432]{0:T(1024)(128)(2,1)}) %all-gather.6.cloned.1.call-update) | async-done | bytes 1572880 | tf_op jit(solution)/shard_map/all_gather | solution.py:108
  40.0 1.8 reshape.110
  41.9 7.2 %slice_reduce_fusion.3 = (bf16[147456]{0:T(1024)(128)(2,1)S(1)}, bf16[147456]{0:T(1024)(128)(2,1)}, bf16[147456]{0:T(1024)(128)(2,1)}, bf16[147456]{0:T(1024)(128)(2,1)S(1)}) fusion(bf16[2,393216]{1,0:T(2,128)(2,1)S(1)} %reshape.110), kind=kLoop, calls=%fused_computation.80 | loop fusion | bytes 2359296 | tf_op jit(solution)/shard_map/slice | solution.py:113
  49.0 1.1 reshape_squeeze.35
  50.1 1.1 reshape_squeeze.34
  51.7 1.4 fusion.49
  53.1 1.4 fusion.48
  55.6 0.6 copy-done.13
  56.9 1.0 pad_maximum_fusion.1
  57.9 1.3 convolution_convert_fusion.3
  59.4 62.0 %all-gather.4.cloned.1.call-done = bf16[4,1536,256]{2,1,0:T(8,128)(2,1)} async-done(((bf16[4,384,256]{2,1,0:T(8,128)(2,1)}), bf16[4,1536,256]{2,1,0:T(8,128)(2,1)}) %all-gather.4.cloned.1.call-update) | async-done | bytes 3145744 | tf_op jit(solution)/shard_map/all_gather | solution.py:131
  121.5 3.3 %fusion.82 = (bf16[1,1536,256]{2,1,0:T(8,128)(2,1)S(1)}, bf16[1,1536,256]{2,1,0:T(8,128)(2,1)}, bf16[1,1536,256]{2,1,0:T(8,128)(2,1)}, bf16[1,1536,256]{2,1,0:T(8,128)(2,1)}) fusion(bf16[4,1536,256]{2,1,0:T(8,128)(2,1)} %all-gather.4.cloned.1.call-done), kind=kLoop, calls=%fused_computation.131 | loop fusion | bytes 6291456 | tf_op jit(solution)/shard_map/slice | solution.py:139
  124.8 11.9 %while.30 = (s32[]{:T(128)}, f32[4,384]{1,0:T(4,128)S(1)}, f32[4,384]{1,0:T(4,128)S(1)}, f32[384,256]{0,1:T(8,128)S(1)}, bf16[2,768,256]{2,1,0:T(8,128)(2,1)}, /...) while((s32[]{:T(128)}, f32[4,384]{1,0:T(4,128)S(1)}, ...), condition=%wide.region_7.8_spmd.clone, body=%wide.region_4.7_spmd.clone.sunk | while | flops 311632896 | bytes 20742316 | solution.py:87
  124.8 0.7 copy-done.6
  125.5 1.2 constant_dynamic-slice_fusion.6
  127.0 1.8 bitcast_reduce_fusion.4
  128.8 1.0 fusion.124
  129.8 0.8 fusion.122
  130.7 0.7 copy-done.6
  131.4 1.2 constant_dynamic-slice_fusion.6
  132.9 1.8 bitcast_reduce_fusion.4
  134.7 1.0 fusion.124
  135.8 0.8 fusion.122
  136.7 2.2 convolution_convert_fusion.1
  139.2 28.6 %all-reduce.4.cloned.1.call-done = bf16[384,768]{1,0:T(8,128)(2,1)} async-done(((bf16[384,768]{1,0:T(8,128)(2,1)}), bf16[384,768]{1,0:T(8,128)(2,1)}) %all-reduce.4.cloned.1.call-update) | async-done | bytes 589840 | tf_op jit(solution)/shard_map/psum | solution.py:135
  167.8 1.3 convert_reduce_fusion
  169.5 1.4 convolution_convert_fusion.2
  171.1 11.6 %while.31 = (s32[]{:T(128)}, f32[4,384]{1,0:T(4,128)S(1)}, f32[4,384]{1,0:T(4,128)S(1)}, f32[384,256]{0,1:T(8,128)S(1)}, bf16[2,768,256]{2,1,0:T(8,128)(2,1)}, /...) while((s32[]{:T(128)}, f32[4,384]{1,0:T(4,128)S(1)}, ...), condition=%wide.region_14.15_spmd.clone, body=%wide.region_11.14_spmd.clone.sunk | while | flops 311632896 | bytes 20742316 | solution.py:87
  171.1 0.7 copy-done.8
  171.8 1.0 constant_dynamic-slice_fusion.7
  173.2 1.8 bitcast_reduce_fusion.5
  175.0 1.0 fusion.132
  176.0 0.8 fusion.130
  176.9 0.7 copy-done.8
  177.6 1.0 constant_dynamic-slice_fusion.7
  179.0 1.8 bitcast_reduce_fusion.5
  180.8 1.0 fusion.132
  181.8 0.8 fusion.130
  182.8 2.3 convolution_convert_fusion
  185.3 30.0 %all-reduce.6.cloned.1.call-done = bf16[384,768]{1,0:T(8,128)(2,1)} async-done(((bf16[384,768]{1,0:T(8,128)(2,1)}), bf16[384,768]{1,0:T(8,128)(2,1)}) %all-reduce.6.cloned.1.call-update) | async-done | bytes 589840 | tf_op jit(solution)/shard_map/psum | solution.py:142
  215.3 1.2 fusion.45
  217.0 3.4 %collective-permute-start = (bf16[1,66,256]{2,1,0:T(8,128)(2,1)S(1)}, bf16[1,66,256]{2,1,0:T(8,128)(2,1)S(1)}, u32[]{:S(2)}, u32[]{:S(2)}) collective-permute-start(bf16[1,66,256]{2,1,0:T(8,128)(2,1)S(1)} %get-tuple-element.212), channel_id=1, source_target_pairs={{0,4},{4,8},{8,12},{1,5},{5,9},{9,13},{2,6},{6,10},{10,14},{3,7},{... | collective-permute-start | bytes 101384 | tf_op jit(solution)/shard_map/ppermute | solution.py:19
  220.4 1.3 collective-permute-start.1
  222.2 4.1 %collective-permute-done.1 = bf16[1,66,256]{2,1,0:T(8,128)(2,1)S(1)} collective-permute-done((bf16[1,66,256]{2,1,0:T(8,128)(2,1)S(1)}, bf16[1,66,256]{2,1,0:T(8,128)(2,1)S(1)}, u32[]{:S(2)}, u32[]{:S(2)}) %collective-permute-start.1) | collective-permute-done | bytes 33824 | tf_op jit(solution)/shard_map/ppermute | solution.py:21
  226.4 1.1 fusion.51
  (105 shorter events, 6.6 us)
Async XLA Ops:
  6.5 219.8 %copy-start = (bf16[3,3,256,256]{3,2,1,0:T(8,128)(2,1)S(1)}, bf16[3,3,256,256]{3,2,1,0:T(8,128)(2,1)}, u32[]{:S(2)}) copy-start(bf16[3,3,256,256]{3,2,1,0:T(8,128)(2,1)} %param.19) | copy-start | bytes 3538948
  6.5 2.3 copy-start.12
  6.5 33.5 %all-gather.6.cloned.1.call-start = ((), (), s32[]{:S(2)}) async-start(), calls=%async_computation.3 | async-start | bytes 2359296 | tf_op jit(solution)/shard_map/all_gather | solution.py:108
  10.0 111.5 %all-gather.4.cloned.1.call-start = ((), (), s32[]{:S(2)}) async-start(), calls=%async_computation | async-start | bytes 3932160 | tf_op jit(solution)/shard_map/all_gather | solution.py:131
  41.8 7.2 %copy-start.1 = (bf16[2,393216]{1,0:T(2,128)(2,1)}, bf16[2,393216]{1,0:T(2,128)(2,1)S(1)}, u32[]{:S(2)}) copy-start(bf16[2,393216]{1,0:T(2,128)(2,1)S(1)} %reshape.110) | copy-start | bytes 4718596
  54.7 0.9 copy-start.2
  54.8 0.8 copy-start.4
  54.8 1.4 copy-start.13
  57.9 110.0 %all-reduce.4.cloned.1.call-start = ((), (), s32[]{:S(2)}) async-start(), calls=%async_computation.1 | async-start | bytes 1179648 | tf_op jit(solution)/shard_map/psum | solution.py:135
  124.8 0.7 copy-start.6
  129.8 0.9 copy-start.7
  130.7 0.7 copy-start.6
  135.7 0.9 copy-start.7
  136.7 31.2 %copy-start.3 = (bf16[384,384]{1,0:T(8,128)(2,1)S(1)}, bf16[384,384]{1,0:T(8,128)(2,1)}, u32[]{:S(2)}) copy-start(bf16[384,384]{1,0:T(8,128)(2,1)} %copy-done.2) | copy-start | bytes 884740
  136.7 31.2 %copy-start.5 = (bf16[384,384]{1,0:T(8,128)(2,1)S(1)}, bf16[384,384]{1,0:T(8,128)(2,1)}, u32[]{:S(2)}) copy-start(bf16[384,384]{1,0:T(8,128)(2,1)} %copy-done.4) | copy-start | bytes 884740
  139.0 76.3 %all-reduce.6.cloned.1.call-start = ((), (), s32[]{:S(2)}) async-start(), calls=%async_computation.2 | async-start | bytes 1179648 | tf_op jit(solution)/shard_map/psum | solution.py:142
  169.2 1.7 copy-start.10
  171.1 0.7 copy-start.8
  176.0 0.9 copy-start.9
  176.9 0.7 copy-start.8
  181.8 0.9 copy-start.9
  182.8 2.3 slice-start
  185.0 30.3 %copy-start.11 = (bf16[384,768]{1,0:T(8,128)(2,1)S(1)}, bf16[384,768]{1,0:T(8,128)(2,1)}, u32[]{:S(2)}) copy-start(bf16[384,768]{1,0:T(8,128)(2,1)} %copy-done.10) | copy-start | bytes 1769476
  217.0 5.0 %collective-permute-start = (bf16[1,66,256]{2,1,0:T(8,128)(2,1)S(1)}, bf16[1,66,256]{2,1,0:T(8,128)(2,1)S(1)}, u32[]{:S(2)}, u32[]{:S(2)}) collective-permute-start(bf16[1,66,256]{2,1,0:T(8,128)(2,1)S(1)} %get-tuple-element.212), channel_id=1, source_target_pairs={{0,4},{4,8},{8,12},{1,5},{5,9},{9,13},{2,6},{6,10},{10,14},{3,7},{... | collective-permute-start | bytes 101384 | tf_op jit(solution)/shard_map/ppermute | solution.py:19
  220.4 5.9 %collective-permute-start.1 = (bf16[1,66,256]{2,1,0:T(8,128)(2,1)S(1)}, bf16[1,66,256]{2,1,0:T(8,128)(2,1)S(1)}, u32[]{:S(2)}, u32[]{:S(2)}) collective-permute-start(bf16[1,66,256]{2,1,0:T(8,128)(2,1)S(1)} %get-tuple-element.211), channel_id=1, source_target_pairs={{4,0},{8,4},{12,8},{5,1},{9,5},{13,9},{6,2},{10,6},{14,10},{7,3},{... | collective-permute-start | bytes 101384 | tf_op jit(solution)/shard_map/ppermute | solution.py:21
Sparse Core Ops, SparseCore 0:
  10.1 29.8 all-gather.5
  58.0 63.4 all-gather.3
  139.1 28.7 all-reduce.3
  185.2 30.0 all-reduce.5

commit v2 on v1

--- a/solution.py
+++ b/solution.py
@@ -96,27 +96,40 @@
     return normalized.reshape(query_count, head_count * HD).astype(jnp.bfloat16)
 
 
+def shifted(value, axis):
+    count = lax.axis_size(axis)
+    return [value] + [
+        lax.ppermute(value, axis, [(i, (i + shift) % count) for i in range(count)])
+        for shift in range(1, count)
+    ]
+
+
+def gather_ordered(value, axis):
+    count = lax.axis_size(axis)
+    stack = jnp.stack(shifted(value, axis))
+    order = (lax.axis_index(axis) - jnp.arange(count)) % count
+    return jnp.take(stack, order, axis=0)
+
+
+def sum_over(value, axis):
+    total = value.astype(jnp.float32)
+    for piece in shifted(value, axis)[1:]:
+        total = total + piece.astype(jnp.float32)
+    return total
+
+
 def body(
     left_tokens, right_tokens, self_qkv, self_out, cross_qkv, cross_out, reassemble, conv_weight
 ):
     tiles = lax.axis_size("tile")
     tile_index = lax.axis_index("tile")
     token_count, feature_share = left_tokens.shape[1], left_tokens.shape[2]
-    packed = jnp.concatenate(
-        [left_tokens[0].reshape(-1), right_tokens[0].reshape(-1), reassemble.reshape(-1)]
-    )
-    gathered = lax.all_gather(packed, "tile", axis=0)
-    block = token_count * feature_share
-
-    def features(offset):
-        return jnp.concatenate(
-            [gathered[i, offset : offset + block].reshape(token_count, feature_share) for i in range(tiles)],
-            axis=1,
-        )
-
-    left_full = features(0)
-    right_full = features(block)
-    reassemble_full = gathered[:, 2 * block :].reshape(tiles * reassemble.shape[0], CH)
+    tokens = gather_ordered(jnp.stack([left_tokens[0], right_tokens[0]]), "tile")
+    left_full, right_full = (
+        jnp.moveaxis(tokens[:, side], 0, 1).reshape(token_count, tiles * feature_share)
+        for side in range(2)
+    )
+    reassemble_full = gather_ordered(reassemble, "tile").reshape(-1, CH)
     left_normed = layer_norm(left_full)
     right_normed = layer_norm(right_full)
     self_query = project_rows(left_normed, self_qkv[0])
@@ -128,18 +141,18 @@
             project_rows(right_normed, cross_qkv[2]),
         ]
     )
-    pieces = lax.all_gather(projected, "blk", axis=1, tiled=True)
+    pieces = jnp.concatenate(shifted(projected, "blk"), axis=1)
     self_state = fold_keys(initial_state(self_query), self_query, pieces[0], pieces[1])
     self_mixed = finish_state(self_state)
     self_term = jnp.dot(self_mixed, self_out, preferred_element_type=jnp.float32)
-    self_sum = lax.psum(self_term.astype(jnp.bfloat16), "tile").astype(jnp.float32)
+    self_sum = sum_over(self_term.astype(jnp.bfloat16), "tile")
     updated = (left_full.astype(jnp.float32) + self_sum).astype(jnp.bfloat16)
     updated_normed = layer_norm(updated)
     cross_query = project_rows(updated_normed, cross_qkv[0])
     cross_state = fold_keys(initial_state(cross_query), cross_query, pieces[2], pieces[3])
     cross_mixed = finish_state(cross_state)
     cross_term = jnp.dot(cross_mixed, cross_out, preferred_element_type=jnp.float32)
-    cross_sum = lax.psum(cross_term.astype(jnp.bfloat16), "tile").astype(jnp.float32)
+    cross_sum = sum_over(cross_term.astype(jnp.bfloat16), "tile")
     final_tokens = (updated.astype(jnp.float32) + cross_sum).astype(jnp.bfloat16)
     band_rows = token_count // GRID_W
     column_count = GRID_W // tiles

time: 235 us -> 209 us (0.89)
  waiting for transfers between devices: 155 us -> 108 us
  matrix products: 23 us -> 41.9 us
  between operations: 13.5 us -> 0.41 us
  starting transfers between devices: 4.99 us -> 18 us
  other arithmetic: 9.46 us -> 20.3 us
  local copies, waits for them, and re-layouts: 27.7 us -> 19.5 us
    ppermute x0 -> x7, waiting for transfers between devices: none -> 103 us  [shifted(): lax.ppermute(value, axis, [(i, (i + shift) % count) for i in range(count)])]
    all_gather x2 -> x0, waiting for transfers between devices: 92 us -> none  [the longest x1 62 us: body(): pieces = lax.all_gather(projected, 'blk', axis=1, tiled=True)]
    psum x2 -> x0, waiting for transfers between devices: 58.6 us -> none  [the longest x1 30 us: body(): lax.psum(cross_term.astype(jnp.bfloat16), 'tile').astype(jnp.float32)]
    ppermute x0 -> x7, starting transfers between devices: none -> 11.6 us  [shifted(): lax.ppermute(value, axis, [(i, (i + shift) % count) for i in range(count)])]
    reduce_sum x4, other arithmetic: 3.15 us -> 12.6 us  [attend_keys(): totals = totals * correction + jnp.sum(expanded, axis=2)]
    dot_general x4, matrix products: 4.05 us -> 13.4 us  [attend_keys(): jnp.einsum('hqk,khd->qhd', expanded.astype(jnp.bfloat16), values_rows.res...]
    dot_general x4, matrix products: 7.05 us -> 15.5 us  [attend_keys(): jnp.einsum('qhd,khd->hqk', queries.reshape(query_count, head_count, HD),...]
    slice x3 -> x0, local copies, waits for them, and re-layouts: 7.19 us -> none  [the longest x1 7.18 us: features(): gathered[i, offset:offset + block].reshape(token_count, feature_share)]
  transfers between devices with their start and end apart: 6 -> 9, of which waited for: 6 -> 7; matrix products, arithmetic and copies ran while one was open for 1% -> 2% of each run, Pallas kernels for 0% -> 0%
where the time goes in v2:
time: 209 us; the launch traced here: 208 us
  waiting for transfers between devices  108 us (52%)
  matrix products  41.9 us (20%)
  other arithmetic  20.3 us (10%)
  local copies, waits for them, and re-layouts  19.5 us (9%)
  starting transfers between devices  18 us (9%)
    ppermute x7, waiting for transfers between devices, shifted(): lax.ppermute(value, axis, [(i, (i + shift) % count) for i in range(count)])  103 us
    dot_general x4, matrix products, attend_keys(): jnp.einsum('qhd,khd->hqk', queries.reshape(query_count, head_count, HD),...  15.5 us
    dot_general x4, matrix products, attend_keys(): jnp.einsum('hqk,khd->qhd', expanded.astype(jnp.bfloat16), values_rows.res...  13.4 us
    reduce_sum x4, other arithmetic, attend_keys(): totals = totals * correction + jnp.sum(expanded, axis=2)  12.6 us
    ppermute x7, starting transfers between devices, shifted(): lax.ppermute(value, axis, [(i, (i + shift) % count) for i in range(count)])  11.6 us
    dot_general x6, matrix products, project_rows(): jnp.dot(normed, weight, preferred_element_type=jnp.float32)  8.89 us
    dynamic_slice x12, local copies, waits for them, and re-layouts, fold_keys(): lax.scan(step_block, running, (stacked_keys, stacked_values))  5.8 us
    ppermute x1, starting transfers between devices, padded_2(): lax.ppermute(tail, axis, [(i, (i + 1) % count) for i in range(ends)])  5.12 us
  transfers between devices with their start and end apart: 9, of which 7 were waited for; matrix products, arithmetic and copies ran while one was open for 2% of the time, Pallas kernels for 0%

profile of v2, /device:TPU:0, one launch (start us, length us, event | category | flops | bytes accessed | tf_op | source)
XLA Modules:
  0.0 208.2 jit_solution(17777016457283811018)
XLA Ops:
  0.0 1.1 constant_dynamic-update-slice_fusion.1
  1.1 1.0 constant_dynamic-update-slice_fusion
  2.1 3.0 %collective-permute-start = (bf16[2,384,384]{2,1,0:T(8,128)(2,1)S(1)}, bf16[2,384,384]{2,1,0:T(8,128)(2,1)S(1)}, u32[]{:S(2)}, u32[]{:S(2)}) collective-permute-start(bf16[2,384,384]{2,1,0:T(8,128)(2,1)S(1)} %constant_dynamic-update-slice_fusion), channel_id=1, source_target_pairs={{0,2},{2,0},{1,3},{3,1},{4,6},{6,4},{5,7},{7,5},{8,10},{10,8},{9,1... | collective-permute-start | bytes 1769480 | tf_op jit(solution)/shard_map/ppermute | solution.py:102
  5.2 13.3 %collective-permute-done = bf16[2,384,384]{2,1,0:T(8,128)(2,1)S(1)} collective-permute-done((bf16[2,384,384]{2,1,0:T(8,128)(2,1)S(1)}, bf16[2,384,384]{2,1,0:T(8,128)(2,1)S(1)}, u32[]{:S(2)}, u32[]{:S(2)}) %collective-permute-start) | collective-permute-done | bytes 589856 | tf_op jit(solution)/shard_map/ppermute | solution.py:102
  20.7 1.1 copy.31
  21.8 1.6 fusion.50
  23.4 1.4 fusion.49
  24.8 1.1 copy.30
  25.9 1.6 fusion.48
  27.5 1.4 fusion.47
  29.8 3.9 %collective-permute-start.3 = (bf16[4,384,256]{2,1,0:T(8,128)(2,1)}, bf16[4,384,256]{2,1,0:T(8,128)(2,1)}, u32[]{:S(2)}, u32[]{:S(2)}) collective-permute-start(bf16[4,384,256]{2,1,0:T(8,128)(2,1)} %pad_maximum_fusion.2), channel_id=1, source_target_pairs={{0,12},{4,0},{8,4},{12,8},{1,13},{5,1},{9,5},{13,9},{2,14},{6,2},{... | collective-permute-start | bytes 2359304 | tf_op jit(solution)/shard_map/ppermute | solution.py:102
  33.7 1.0 collective-permute-start.1
  34.7 1.5 convolution_convert_fusion.3
  37.1 14.9 %collective-permute-done.3 = bf16[4,384,256]{2,1,0:T(8,128)(2,1)} collective-permute-done((bf16[4,384,256]{2,1,0:T(8,128)(2,1)}, bf16[4,384,256]{2,1,0:T(8,128)(2,1)}, u32[]{:S(2)}, u32[]{:S(2)}) %collective-permute-start.3) | collective-permute-done | bytes 786464 | tf_op jit(solution)/shard_map/ppermute | solution.py:102
  52.0 48.4 %collective-permute-done.2 = bf16[4,384,256]{2,1,0:T(8,128)(2,1)} collective-permute-done((bf16[4,384,256]{2,1,0:T(8,128)(2,1)}, bf16[4,384,256]{2,1,0:T(8,128)(2,1)}, u32[]{:S(2)}, u32[]{:S(2)}) %collective-permute-start.2) | collective-permute-done | bytes 786464 | tf_op jit(solution)/shard_map/ppermute | solution.py:102
  100.4 1.9 pad_maximum_fusion
  102.3 1.7 fusion.85
  104.8 26.8 %while.30 = (s32[]{:T(128)}, f32[4,384]{1,0:T(4,128)}, f32[4,384]{1,0:T(4,128)}, f32[384,256]{0,1:T(8,128)}, bf16[2,768,256]{2,1,0:T(8,128)(2,1)}, /*index=5*/bf...) while((s32[]{:T(128)}, f32[4,384]{1,0:T(4,128)}, f32[4,384]{1,0:T(4,128)}, ...), condition=%wide.region_7.8_spmd.clone, body=%wide.region_4.7_spmd.clone.sunk | while | flops 311632896 | bytes 22388992 | solution.py:87
  104.8 1.2 constant_dynamic-slice_fusion.6
  106.2 3.9 %bitcast_reduce_fusion.4 = (f32[4,384]{1,0:T(4,128)S(1)}, f32[4,768,384]{2,1,0:T(8,128)}) fusion(bf16[768,4,64]{0,2,1:T(8,128)(2,1)S(1)} %bitcast.216, bf16[384,4,64]{0,2,1:T(8,128)(2,1)} %bitcast.226), kind=kOutput, calls=%fused_computation.3.clone.1 | convolution fusion | flops 153352704 | bytes 5314560 | tf_op jit(solution)/shard_map/while/body/eval_jaxpr/qhd,khd->hqk/dot_general | solution.py:54
  110.1 3.2 %fusion.127 = f32[4,384]{1,0:T(4,128)S(1)} fusion(f32[4,768,384]{2,1,0:T(8,128)} %get-tuple-element.325, f32[4,384]{1,0:T(4,128)S(1)} %get-tuple-element.360), kind=kLoop, calls=%fused_computation.6.clone.1 | loop fusion | flops 3537408 | bytes 4730880 | tf_op jit(solution)/shard_map/while/body/eval_jaxpr/reduce_sum | solution.py:63
  114.1 3.3 %fusion.129 = f32[384,4,64]{0,2,1:T(8,128)S(1)} fusion(bf16[768,4,64]{0,2,1:T(8,128)(2,1)S(1)} %bitcast.214, f32[4,768,384]{2,1,0:T(8,128)} %get-tuple-element.325, f32[4,384]{1,0:T(4,128)S(1)} %get-tuple-element.360, f32[384,4,64]{0,2,1:T(8,128)S(1)} %bitcast.220, f32[384,4]{0,1:T(4,128)S(1)} %get-tuple-element.327), kind=kOutput, calls=%fused_computation.11.clone.1 | convolution fusion | flops 154730496 | bytes 5910528 | tf_op jit(solution)/shard_map/while/body/eval_jaxpr/hqk,khd->qhd/dot_general | solution.py:64
  118.2 1.2 constant_dynamic-slice_fusion.6
  119.6 3.9 %bitcast_reduce_fusion.4 = (f32[4,384]{1,0:T(4,128)S(1)}, f32[4,768,384]{2,1,0:T(8,128)}) fusion(bf16[768,4,64]{0,2,1:T(8,128)(2,1)S(1)} %bitcast.216, bf16[384,4,64]{0,2,1:T(8,128)(2,1)} %bitcast.226), kind=kOutput, calls=%fused_computation.3.clone.1 | convolution fusion | flops 153352704 | bytes 5314560 | tf_op jit(solution)/shard_map/while/body/eval_jaxpr/qhd,khd->hqk/dot_general | solution.py:54
  123.5 3.2 %fusion.127 = f32[4,384]{1,0:T(4,128)S(1)} fusion(f32[4,768,384]{2,1,0:T(8,128)} %get-tuple-element.325, f32[4,384]{1,0:T(4,128)S(1)} %get-tuple-element.360), kind=kLoop, calls=%fused_computation.6.clone.1 | loop fusion | flops 3537408 | bytes 4730880 | tf_op jit(solution)/shard_map/while/body/eval_jaxpr/reduce_sum | solution.py:63
  127.5 3.3 %fusion.129 = f32[384,4,64]{0,2,1:T(8,128)S(1)} fusion(bf16[768,4,64]{0,2,1:T(8,128)(2,1)S(1)} %bitcast.214, f32[4,768,384]{2,1,0:T(8,128)} %get-tuple-element.325, f32[4,384]{1,0:T(4,128)S(1)} %get-tuple-element.360, f32[384,4,64]{0,2,1:T(8,128)S(1)} %bitcast.220, f32[384,4]{0,1:T(4,128)S(1)} %get-tuple-element.327), kind=kOutput, calls=%fused_computation.11.clone.1 | convolution fusion | flops 154730496 | bytes 5910528 | tf_op jit(solution)/shard_map/while/body/eval_jaxpr/hqk,khd->qhd/dot_general | solution.py:64
  131.6 1.0 fusion.60
  132.6 1.4 convolution_convert_fusion.1
  134.0 1.6 collective-permute-start.4
  135.7 11.7 %collective-permute-done.4 = bf16[384,768]{1,0:T(8,128)(2,1)S(1)} collective-permute-done((bf16[384,768]{1,0:T(8,128)(2,1)S(1)}, bf16[384,768]{1,0:T(8,128)(2,1)S(1)}, u32[]{:S(2)}, u32[]{:S(2)}) %collective-permute-start.4) | collective-permute-done | bytes 589856 | tf_op jit(solution)/shard_map/ppermute | solution.py:102
  148.6 1.4 convolution_convert_fusion.2
  150.9 23.6 %while.31 = (s32[]{:T(128)}, f32[4,384]{1,0:T(4,128)S(1)}, f32[4,384]{1,0:T(4,128)S(1)}, f32[384,256]{0,1:T(8,128)S(1)}, bf16[2,768,256]{2,1,0:T(8,128)(2,1)}, /...) while((s32[]{:T(128)}, f32[4,384]{1,0:T(4,128)S(1)}, ...), condition=%wide.region_13.14_spmd.clone, body=%wide.region_10.13_spmd.clone.sunk | while | flops 311632896 | bytes 19169396 | solution.py:87
  150.9 1.1 constant_dynamic-slice_fusion.7
  152.1 3.9 %bitcast_reduce_fusion.5 = (f32[4,384]{1,0:T(4,128)S(1)}, f32[4,768,384]{2,1,0:T(8,128)}) fusion(bf16[768,4,64]{0,2,1:T(8,128)(2,1)S(1)} %bitcast.217, bf16[384,4,64]{0,2,1:T(8,128)(2,1)} %bitcast.227), kind=kOutput, calls=%fused_computation.21.clone.1 | convolution fusion | flops 153352704 | bytes 5314560 | tf_op jit(solution)/shard_map/while/body/eval_jaxpr/qhd,khd->hqk/dot_general | solution.py:54
  156.0 3.1 %fusion.135 = f32[4,384]{1,0:T(4,128)S(1)} fusion(f32[4,768,384]{2,1,0:T(8,128)} %get-tuple-element.338, f32[4,384]{1,0:T(4,128)S(1)} %get-tuple-element.387), kind=kLoop, calls=%fused_computation.24.clone.1 | loop fusion | flops 3537408 | bytes 4730880 | tf_op jit(solution)/shard_map/while/body/eval_jaxpr/reduce_sum | solution.py:63
  159.3 3.3 %fusion.137 = f32[384,4,64]{0,2,1:T(8,128)S(1)} fusion(bf16[768,4,64]{0,2,1:T(8,128)(2,1)S(1)} %bitcast.215, f32[4,768,384]{2,1,0:T(8,128)} %get-tuple-element.338, f32[4,384]{1,0:T(4,128)S(1)} %get-tuple-element.387, f32[384,4,64]{0,2,1:T(8,128)S(1)} %bitcast.218, f32[384,4]{0,1:T(4,128)S(1)} %get-tuple-element.340), kind=kOutput, calls=%fused_computation.29.clone.1 | convolution fusion | flops 154730496 | bytes 5910528 | tf_op jit(solution)/shard_map/while/body/eval_jaxpr/hqk,khd->qhd/dot_general | solution.py:64
  162.7 1.1 constant_dynamic-slice_fusion.7
  163.9 3.9 %bitcast_reduce_fusion.5 = (f32[4,384]{1,0:T(4,128)S(1)}, f32[4,768,384]{2,1,0:T(8,128)}) fusion(bf16[768,4,64]{0,2,1:T(8,128)(2,1)S(1)} %bitcast.217, bf16[384,4,64]{0,2,1:T(8,128)(2,1)} %bitcast.227), kind=kOutput, calls=%fused_computation.21.clone.1 | convolution fusion | flops 153352704 | bytes 5314560 | tf_op jit(solution)/shard_map/while/body/eval_jaxpr/qhd,khd->hqk/dot_general | solution.py:54
  167.8 3.1 %fusion.135 = f32[4,384]{1,0:T(4,128)S(1)} fusion(f32[4,768,384]{2,1,0:T(8,128)} %get-tuple-element.338, f32[4,384]{1,0:T(4,128)S(1)} %get-tuple-element.387), kind=kLoop, calls=%fused_computation.24.clone.1 | loop fusion | flops 3537408 | bytes 4730880 | tf_op jit(solution)/shard_map/while/body/eval_jaxpr/reduce_sum | solution.py:63
  171.2 3.3 %fusion.137 = f32[384,4,64]{0,2,1:T(8,128)S(1)} fusion(bf16[768,4,64]{0,2,1:T(8,128)(2,1)S(1)} %bitcast.215, f32[4,768,384]{2,1,0:T(8,128)} %get-tuple-element.338, f32[4,384]{1,0:T(4,128)S(1)} %get-tuple-element.387, f32[384,4,64]{0,2,1:T(8,128)S(1)} %bitcast.218, f32[384,4]{0,1:T(4,128)S(1)} %get-tuple-element.340), kind=kOutput, calls=%fused_computation.29.clone.1 | convolution fusion | flops 154730496 | bytes 5910528 | tf_op jit(solution)/shard_map/while/body/eval_jaxpr/hqk,khd->qhd/dot_general | solution.py:64
  174.6 1.4 convolution_convert_fusion
  176.0 1.6 collective-permute-start.5
  178.1 14.7 %collective-permute-done.6 = bf16[384,256]{1,0:T(8,128)(2,1)S(1)} collective-permute-done((bf16[384,256]{1,0:T(8,128)(2,1)S(1)}, bf16[384,256]{1,0:T(8,128)(2,1)S(1)}, u32[]{:S(2)}, u32[]{:S(2)}) %collective-permute-start.6) | collective-permute-done | bytes 196640 | tf_op jit(solution)/shard_map/ppermute | solution.py:102
  193.8 1.3 fusion.41
  195.6 5.1 %collective-permute-start.7 = (bf16[1,66,256]{2,1,0:T(8,128)(2,1)S(1)}, bf16[1,66,256]{2,1,0:T(8,128)(2,1)S(1)}, u32[]{:S(2)}, u32[]{:S(2)}) collective-permute-start(bf16[1,66,256]{2,1,0:T(8,128)(2,1)S(1)} %get-tuple-element.228), channel_id=1, source_target_pairs={{0,4},{4,8},{8,12},{1,5},{5,9},{9,13},{2,6},{6,10},{10,14},{3,7},{... | collective-permute-start | bytes 101384 | tf_op jit(solution)/shard_map/ppermute | solution.py:19
  200.8 1.3 collective-permute-start.8
  202.5 4.5 %collective-permute-done.8 = bf16[1,66,256]{2,1,0:T(8,128)(2,1)S(1)} collective-permute-done((bf16[1,66,256]{2,1,0:T(8,128)(2,1)S(1)}, bf16[1,66,256]{2,1,0:T(8,128)(2,1)S(1)}, u32[]{:S(2)}, u32[]{:S(2)}) %collective-permute-start.8) | collective-permute-done | bytes 33824 | tf_op jit(solution)/shard_map/ppermute | solution.py:21
  207.2 1.1 fusion.52
  (111 shorter events, 13.8 us)
Async XLA Ops:
  0.0 207.2 %copy-start = (bf16[3,3,256,256]{3,2,1,0:T(8,128)(2,1)S(1)}, bf16[3,3,256,256]{3,2,1,0:T(8,128)(2,1)}, u32[]{:S(2)}) copy-start(bf16[3,3,256,256]{3,2,1,0:T(8,128)(2,1)} %param.19) | copy-start | bytes 3538948
  2.1 16.4 %collective-permute-start = (bf16[2,384,384]{2,1,0:T(8,128)(2,1)S(1)}, bf16[2,384,384]{2,1,0:T(8,128)(2,1)S(1)}, u32[]{:S(2)}, u32[]{:S(2)}) collective-permute-start(bf16[2,384,384]{2,1,0:T(8,128)(2,1)S(1)} %constant_dynamic-update-slice_fusion), channel_id=1, source_target_pairs={{0,2},{2,0},{1,3},{3,1},{4,6},{6,4},{5,7},{7,5},{8,10},{10,8},{9,1... | collective-permute-start | bytes 1769480 | tf_op jit(solution)/shard_map/ppermute | solution.py:102
  5.2 14.3 %copy-start.13 = (pred[2]{0:T(512)(128)(4,1)}, pred[2]{0:T(512)(128)(4,1)S(1)}, u32[]{:S(2)}) copy-start(pred[2]{0:T(512)(128)(4,1)S(1)} %compare_and_fusion) | copy-start | bytes 10
  5.2 13.4 %copy-start.12 = (s32[1024]{0:T(1024)}, s32[1024]{0:T(1024)S(1)}, u32[]{:S(2)}) copy-start(s32[1024]{0:T(1024)S(1)} %pad_clamp_fusion) | copy-start | bytes 12292
  21.8 1.6 copy-start.8
  25.9 1.6 copy-start.7
  29.8 22.1 %collective-permute-start.3 = (bf16[4,384,256]{2,1,0:T(8,128)(2,1)}, bf16[4,384,256]{2,1,0:T(8,128)(2,1)}, u32[]{:S(2)}, u32[]{:S(2)}) collective-permute-start(bf16[4,384,256]{2,1,0:T(8,128)(2,1)} %pad_maximum_fusion.2), channel_id=1, source_target_pairs={{0,12},{4,0},{8,4},{12,8},{1,13},{5,1},{9,5},{13,9},{2,14},{6,2},{... | collective-permute-start | bytes 2359304 | tf_op jit(solution)/shard_map/ppermute | solution.py:102
  33.7 66.7 %collective-permute-start.2 = (bf16[4,384,256]{2,1,0:T(8,128)(2,1)}, bf16[4,384,256]{2,1,0:T(8,128)(2,1)}, u32[]{:S(2)}, u32[]{:S(2)}) collective-permute-start(bf16[4,384,256]{2,1,0:T(8,128)(2,1)} %pad_maximum_fusion.2), channel_id=1, source_target_pairs={{0,8},{4,12},{8,0},{12,4},{1,9},{5,13},{9,1},{13,5},{2,10},{6,14},... | collective-permute-start | bytes 2359304 | tf_op jit(solution)/shard_map/ppermute | solution.py:102
  33.7 66.7 %collective-permute-start.1 = (bf16[4,384,256]{2,1,0:T(8,128)(2,1)}, bf16[4,384,256]{2,1,0:T(8,128)(2,1)}, u32[]{:S(2)}, u32[]{:S(2)}) collective-permute-start(bf16[4,384,256]{2,1,0:T(8,128)(2,1)} %pad_maximum_fusion.2), channel_id=1, source_target_pairs={{0,4},{4,8},{8,12},{12,0},{1,5},{5,9},{9,13},{13,1},{2,6},{6,10},{... | collective-permute-start | bytes 2359304 | tf_op jit(solution)/shard_map/ppermute | solution.py:102
  106.1 3.9 %copy-start.6 = (f32[4,384]{1,0:T(4,128)S(1)}, f32[4,384]{1,0:T(4,128)}, u32[]{:S(2)}) copy-start(f32[4,384]{1,0:T(4,128)} %get-tuple-element.351) | copy-start | bytes 18436 | tf_op jit(solution)/shard_map/while
  110.1 3.2 %copy-start.9 = (f32[4,384]{1,0:T(4,128)S(1)}, f32[4,384]{1,0:T(4,128)}, u32[]{:S(2)}) copy-start(f32[4,384]{1,0:T(4,128)} %get-tuple-element.352) | copy-start | bytes 18436 | tf_op jit(solution)/shard_map/while
  110.1 4.0 %copy-start.1 = (f32[384,256]{0,1:T(8,128)S(1)}, f32[384,256]{0,1:T(8,128)}, u32[]{:S(2)}) copy-start(f32[384,256]{0,1:T(8,128)} %get-tuple-element.353) | copy-start | bytes 1179652 | tf_op jit(solution)/shard_map/while
  113.3 0.6 copy-start.10
  117.4 0.8 copy-start.2
  119.5 3.9 %copy-start.6 = (f32[4,384]{1,0:T(4,128)S(1)}, f32[4,384]{1,0:T(4,128)}, u32[]{:S(2)}) copy-start(f32[4,384]{1,0:T(4,128)} %get-tuple-element.351) | copy-start | bytes 18436 | tf_op jit(solution)/shard_map/while
  123.5 3.2 %copy-start.9 = (f32[4,384]{1,0:T(4,128)S(1)}, f32[4,384]{1,0:T(4,128)}, u32[]{:S(2)}) copy-start(f32[4,384]{1,0:T(4,128)} %get-tuple-element.352) | copy-start | bytes 18436 | tf_op jit(solution)/shard_map/while
  123.5 4.0 %copy-start.1 = (f32[384,256]{0,1:T(8,128)S(1)}, f32[384,256]{0,1:T(8,128)}, u32[]{:S(2)}) copy-start(f32[384,256]{0,1:T(8,128)} %get-tuple-element.353) | copy-start | bytes 1179652 | tf_op jit(solution)/shard_map/while
  126.7 0.6 copy-start.10
  130.8 0.8 copy-start.2
  134.0 13.4 %collective-permute-start.4 = (bf16[384,768]{1,0:T(8,128)(2,1)S(1)}, bf16[384,768]{1,0:T(8,128)(2,1)S(1)}, u32[]{:S(2)}, u32[]{:S(2)}) collective-permute-start(bf16[384,768]{1,0:T(8,128)(2,1)S(1)} %convolution_convert_fusion.1), channel_id=1, source_target_pairs={{0,2},{2,0},{1,3},{3,1},{4,6},{6,4},{5,7},{7,5},{8,10},{10,8},{9,1... | collective-permute-start | bytes 1769480 | tf_op jit(solution)/shard_map/ppermute | solution.py:102
  147.7 0.8 copy-start.4
  148.6 2.3 %copy-start.3 = (bf16[1,1536,256]{2,1,0:T(8,128)(2,1)S(1)}, bf16[1,1536,256]{2,1,0:T(8,128)(2,1)}, u32[]{:S(2)}) copy-start(bf16[1,1536,256]{2,1,0:T(8,128)(2,1)} %get-tuple-element.221) | copy-start | bytes 2359300
  174.5 3.0 %copy-start.11 = (bf16[384,256]{1,0:T(8,128)(2,1)S(1)}, bf16[384,256]{1,0:T(8,128)(2,1)}, u32[]{:S(2)}) copy-start(bf16[384,256]{1,0:T(8,128)(2,1)} %param.18) | copy-start | bytes 589828
  174.6 19.1 %copy-start.14 = (pred[2]{0:T(512)(128)(4,1)S(1)}, pred[2]{0:T(512)(128)(4,1)}, u32[]{:S(2)}) copy-start(pred[2]{0:T(512)(128)(4,1)} %copy-done.13) | copy-start | bytes 10
  176.0 17.8 %collective-permute-start.5 = (bf16[384,768]{1,0:T(8,128)(2,1)S(1)}, bf16[384,768]{1,0:T(8,128)(2,1)}, u32[]{:S(2)}, u32[]{:S(2)}) collective-permute-start(bf16[384,768]{1,0:T(8,128)(2,1)S(1)} %convolution_convert_fusion), channel_id=1, source_target_pairs={{0,2},{2,0},{1,3},{3,1},{4,6},{6,4},{5,7},{7,5},{8,10},{10,8},{9,1... | collective-permute-start | bytes 1769480 | tf_op jit(solution)/shard_map/ppermute | solution.py:102
  177.5 15.2 %collective-permute-start.6 = (bf16[384,256]{1,0:T(8,128)(2,1)S(1)}, bf16[384,256]{1,0:T(8,128)(2,1)S(1)}, u32[]{:S(2)}, u32[]{:S(2)}) collective-permute-start(bf16[384,256]{1,0:T(8,128)(2,1)S(1)} %copy-done.11), channel_id=1, source_target_pairs={{0,2},{2,0},{1,3},{3,1},{4,6},{6,4},{5,7},{7,5},{8,10},{10,8},{9,1... | collective-permute-start | bytes 589832 | tf_op jit(solution)/shard_map/ppermute | solution.py:102
  192.8 1.1 copy-start.5
  195.6 6.7 %collective-permute-start.7 = (bf16[1,66,256]{2,1,0:T(8,128)(2,1)S(1)}, bf16[1,66,256]{2,1,0:T(8,128)(2,1)S(1)}, u32[]{:S(2)}, u32[]{:S(2)}) collective-permute-start(bf16[1,66,256]{2,1,0:T(8,128)(2,1)S(1)} %get-tuple-element.228), channel_id=1, source_target_pairs={{0,4},{4,8},{8,12},{1,5},{5,9},{9,13},{2,6},{6,10},{10,14},{3,7},{... | collective-permute-start | bytes 101384 | tf_op jit(solution)/shard_map/ppermute | solution.py:19
  200.8 6.3 %collective-permute-start.8 = (bf16[1,66,256]{2,1,0:T(8,128)(2,1)S(1)}, bf16[1,66,256]{2,1,0:T(8,128)(2,1)S(1)}, u32[]{:S(2)}, u32[]{:S(2)}) collective-permute-start(bf16[1,66,256]{2,1,0:T(8,128)(2,1)S(1)} %get-tuple-element.227), channel_id=1, source_target_pairs={{4,0},{8,4},{12,8},{5,1},{9,5},{13,9},{6,2},{10,6},{14,10},{7,3},{... | collective-permute-start | bytes 101384 | tf_op jit(solution)/shard_map/ppermute | solution.py:21

commit v3 on v2

--- a/solution.py
+++ b/solution.py
@@ -133,23 +133,26 @@
     left_normed = layer_norm(left_full)
     right_normed = layer_norm(right_full)
     self_query = project_rows(left_normed, self_qkv[0])
-    projected = jnp.stack(
-        [
-            project_rows(left_normed, self_qkv[1]),
-            project_rows(left_normed, self_qkv[2]),
-            project_rows(right_normed, cross_qkv[1]),
-            project_rows(right_normed, cross_qkv[2]),
-        ]
-    )
-    pieces = jnp.concatenate(shifted(projected, "blk"), axis=1)
-    self_state = fold_keys(initial_state(self_query), self_query, pieces[0], pieces[1])
+    self_pieces = shifted(
+        jnp.stack([project_rows(left_normed, self_qkv[1]), project_rows(left_normed, self_qkv[2])]),
+        "blk",
+    )
+    cross_pieces = shifted(
+        jnp.stack([project_rows(right_normed, cross_qkv[1]), project_rows(right_normed, cross_qkv[2])]),
+        "blk",
+    )
+    self_state = initial_state(self_query)
+    for piece in self_pieces:
+        self_state = attend_keys(self_state, self_query, piece[0], piece[1])
     self_mixed = finish_state(self_state)
     self_term = jnp.dot(self_mixed, self_out, preferred_element_type=jnp.float32)
     self_sum = sum_over(self_term.astype(jnp.bfloat16), "tile")
     updated = (left_full.astype(jnp.float32) + self_sum).astype(jnp.bfloat16)
     updated_normed = layer_norm(updated)
     cross_query = project_rows(updated_normed, cross_qkv[0])
-    cross_state = fold_keys(initial_state(cross_query), cross_query, pieces[2], pieces[3])
+    cross_state = initial_state(cross_query)
+    for piece in cross_pieces:
+        cross_state = attend_keys(cross_state, cross_query, piece[0], piece[1])
     cross_mixed = finish_state(cross_state)
     cross_term = jnp.dot(cross_mixed, cross_out, preferred_element_type=jnp.float32)
     cross_sum = sum_over(cross_term.astype(jnp.bfloat16), "tile")

time: 209 us -> 143 us (0.68)
  waiting for transfers between devices: 108 us -> 71.9 us
  matrix products: 41.9 us -> 20.2 us
  starting transfers between devices: 18 us -> 31 us
  other arithmetic: 20.3 us -> 8.64 us
  local copies, waits for them, and re-layouts: 19.5 us -> 9.78 us
    ppermute x7 -> x10, waiting for transfers between devices: 103 us -> 67.5 us  [shifted(): lax.ppermute(value, axis, [(i, (i + shift) % count) for i in range(count)])]
    dot_general x4 -> x8, matrix products: 15.5 us -> 4.26 us  [attend_keys(): jnp.einsum('qhd,khd->hqk', queries.reshape(query_count, head_count, HD),...]
    reduce_sum x4 -> x8, other arithmetic: 12.6 us -> 3.24 us  [attend_keys(): totals = totals * correction + jnp.sum(expanded, axis=2)]
    dot_general x4 -> x8, matrix products: 13.4 us -> 4.4 us  [attend_keys(): jnp.einsum('hqk,khd->qhd', expanded.astype(jnp.bfloat16), values_rows.res...]
    ppermute x1, starting transfers between devices: 5.12 us -> 13.1 us  [padded_2(): lax.ppermute(tail, axis, [(i, (i + 1) % count) for i in range(ends)])]
    dynamic_slice x12 -> x0, local copies, waits for them, and re-layouts: 5.8 us -> none  [fold_keys(): lax.scan(step_block, running, (stacked_keys, stacked_values))]
    ppermute x7 -> x10, starting transfers between devices: 11.6 us -> 16.6 us  [shifted(): lax.ppermute(value, axis, [(i, (i + shift) % count) for i in range(count)])]
    while x24 -> x0, local copies, waits for them, and re-layouts: 2.76 us -> none
  transfers between devices with their start and end apart: 9 -> 12, of which waited for: 7 -> 7; matrix products, arithmetic and copies ran while one was open for 2% -> 11% of each run, Pallas kernels for 0% -> 0%
where the time goes in v3:
time: 143 us; the launch traced here: 142 us
  waiting for transfers between devices  71.9 us (50%)
  starting transfers between devices  31 us (22%)
  matrix products  20.2 us (14%)
  local copies, waits for them, and re-layouts  9.78 us (7%)
  other arithmetic  8.64 us (6%)
    ppermute x10, waiting for transfers between devices, shifted(): lax.ppermute(value, axis, [(i, (i + shift) % count) for i in range(count)])  67.5 us
    ppermute x10, starting transfers between devices, shifted(): lax.ppermute(value, axis, [(i, (i + shift) % count) for i in range(count)])  16.6 us
    ppermute x1, starting transfers between devices, padded_2(): lax.ppermute(tail, axis, [(i, (i + 1) % count) for i in range(ends)])  13.1 us
    dot_general x6, matrix products, project_rows(): jnp.dot(normed, weight, preferred_element_type=jnp.float32)  9.48 us
    dot_general x8, matrix products, attend_keys(): jnp.einsum('hqk,khd->qhd', expanded.astype(jnp.bfloat16), values_rows.res...  4.4 us
    dot_general x8, matrix products, attend_keys(): jnp.einsum('qhd,khd->hqk', queries.reshape(query_count, head_count, HD),...  4.26 us
    ppermute x1, waiting for transfers between devices, padded_2(): lax.ppermute(head, axis, [((i + 1) % count, i) for i in range(ends)])  4.07 us
    reduce_sum x8, other arithmetic, attend_keys(): totals = totals * correction + jnp.sum(expanded, axis=2)  3.24 us
  transfers between devices with their start and end apart: 12, of which 7 were waited for; matrix products, arithmetic and copies ran while one was open for 11% of the time, Pallas kernels for 0%

profile of v3, /device:TPU:0, one launch (start us, length us, event | category | flops | bytes accessed | tf_op | source)
XLA Modules:
  0.0 142.0 jit_solution(8897401653116228344)
XLA Ops:
  0.0 1.1 constant_dynamic-update-slice_fusion.1
  1.1 1.0 constant_dynamic-update-slice_fusion
  2.1 3.0 %collective-permute-start = (bf16[2,384,384]{2,1,0:T(8,128)(2,1)S(1)}, bf16[2,384,384]{2,1,0:T(8,128)(2,1)S(1)}, u32[]{:S(2)}, u32[]{:S(2)}) collective-permute-start(bf16[2,384,384]{2,1,0:T(8,128)(2,1)S(1)} %constant_dynamic-update-slice_fusion), channel_id=1, source_target_pairs={{0,2},{2,0},{1,3},{3,1},{4,6},{6,4},{5,7},{7,5},{8,10},{10,8},{9,1... | collective-permute-start | bytes 1769480 | tf_op jit(solution)/shard_map/ppermute | solution.py:102
  5.2 13.3 %collective-permute-done = bf16[2,384,384]{2,1,0:T(8,128)(2,1)S(1)} collective-permute-done((bf16[2,384,384]{2,1,0:T(8,128)(2,1)S(1)}, bf16[2,384,384]{2,1,0:T(8,128)(2,1)S(1)}, u32[]{:S(2)}, u32[]{:S(2)}) %collective-permute-start) | collective-permute-done | bytes 589856 | tf_op jit(solution)/shard_map/ppermute | solution.py:102
  18.6 0.8 gather_fusion
  20.4 1.1 fusion.80
  21.8 1.4 convolution_convert_fusion.6
  23.3 1.5 %convolution_convert_fusion.5 = bf16[384,256]{0,1:T(8,128)(2,1)S(1)} fusion(bf16[384,768]{0,1:T(8,128)(2,1)S(1)} %bitcast.345, bf16[3,768,256]{2,1,0:T(8,128)(2,1)} %param.10), kind=kOutput, calls=%fused_computation.107 | convolution fusion | flops 151093248 | bytes 1179648 | tf_op jit(solution)/shard_map/dot_general | solution.py:36
  24.8 2.2 %convolution_convert_fusion.7 = bf16[384,256]{0,1:T(8,128)(2,1)} fusion(bf16[384,768]{0,1:T(8,128)(2,1)S(1)} %bitcast.346, bf16[3,768,256]{2,1,0:T(8,128)(2,1)} %param.10), kind=kOutput, calls=%fused_computation.109 | convolution fusion | flops 151093248 | bytes 1179648 | tf_op jit(solution)/shard_map/dot_general | solution.py:36
  26.9 0.8 pad_maximum_fusion.1
  27.7 1.8 %collective-permute-start.1 = (bf16[2,384,256]{1,2,0:T(8,128)(2,1)}, bf16[2,384,256]{1,2,0:T(8,128)(2,1)}, u32[]{:S(2)}, u32[]{:S(2)}) collective-permute-start(bf16[2,384,256]{1,2,0:T(8,128)(2,1)} %pad_maximum_fusion.1), channel_id=1, source_target_pairs={{0,4},{4,8},{8,12},{12,0},{1,5},{5,9},{9,13},{13,1},{2,6},{6,10},{... | collective-permute-start | bytes 1179656 | tf_op jit(solution)/shard_map/ppermute | solution.py:102
  29.6 2.6 %collective-permute-start.2 = (bf16[2,384,256]{1,2,0:T(8,128)(2,1)}, bf16[2,384,256]{1,2,0:T(8,128)(2,1)}, u32[]{:S(2)}, u32[]{:S(2)}) collective-permute-start(bf16[2,384,256]{1,2,0:T(8,128)(2,1)} %pad_maximum_fusion.1), channel_id=1, source_target_pairs={{0,8},{4,12},{8,0},{12,4},{1,9},{5,13},{9,1},{13,5},{2,10},{6,14},... | collective-permute-start | bytes 1179656 | tf_op jit(solution)/shard_map/ppermute | solution.py:102
  32.1 1.3 collective-permute-start.3
  33.6 1.4 copy.33
  35.0 1.4 convolution_convert_fusion.3
  36.4 1.5 %convolution_convert_fusion.2 = bf16[384,256]{0,1:T(8,128)(2,1)S(1)} fusion(bf16[384,768]{0,1:T(8,128)(2,1)S(1)} %bitcast.348, bf16[3,768,256]{2,1,0:T(8,128)(2,1)} %param.12), kind=kOutput, calls=%fused_computation.104 | convolution fusion | flops 151093248 | bytes 1179648 | tf_op jit(solution)/shard_map/dot_general | solution.py:36
  37.9 0.7 collective-permute-start.5
  39.6 2.4 %collective-permute-done.1 = bf16[2,384,256]{1,2,0:T(8,128)(2,1)} collective-permute-done((bf16[2,384,256]{1,2,0:T(8,128)(2,1)}, bf16[2,384,256]{1,2,0:T(8,128)(2,1)}, u32[]{:S(2)}, u32[]{:S(2)}) %collective-permute-start.1) | collective-permute-done | bytes 393248 | tf_op jit(solution)/shard_map/ppermute | solution.py:102
  42.0 2.9 %collective-permute-start.7 = (bf16[2,384,256]{1,2,0:T(8,128)(2,1)S(1)}, bf16[2,384,256]{1,2,0:T(8,128)(2,1)S(1)}, u32[]{:S(2)}, u32[]{:S(2)}) collective-permute-start(bf16[2,384,256]{1,2,0:T(8,128)(2,1)S(1)} %pad_maximum_fusion.2), channel_id=1, source_target_pairs={{0,12},{4,0},{8,4},{12,8},{1,13},{5,1},{9,5},{13,9},{2,14},{6,2},{... | collective-permute-start | bytes 1179656 | tf_op jit(solution)/shard_map/ppermute | solution.py:102
  44.9 1.1 fusion.144
  46.5 12.4 %collective-permute-done.2 = bf16[2,384,256]{1,2,0:T(8,128)(2,1)} collective-permute-done((bf16[2,384,256]{1,2,0:T(8,128)(2,1)}, bf16[2,384,256]{1,2,0:T(8,128)(2,1)}, u32[]{:S(2)}, u32[]{:S(2)}) %collective-permute-start.2) | collective-permute-done | bytes 393248 | tf_op jit(solution)/shard_map/ppermute | solution.py:102
  58.9 1.1 fusion.143
  60.0 0.5 multiply_reduce_fusion.5
  60.5 1.1 fusion.142
  61.6 0.5 multiply_reduce_fusion.4
  63.9 0.5 fusion.26
  64.4 0.6 fusion.27
  65.0 0.5 fusion.28
  65.5 0.6 fusion.74
  66.9 1.8 %collective-permute-start.4 = (bf16[384,768]{1,0:T(8,128)(2,1)S(1)}, bf16[384,768]{1,0:T(8,128)(2,1)S(1)}, u32[]{:S(2)}, u32[]{:S(2)}) collective-permute-start(bf16[384,768]{1,0:T(8,128)(2,1)S(1)} %convolution_convert_fusion.1), channel_id=1, source_target_pairs={{0,2},{2,0},{1,3},{3,1},{4,6},{6,4},{5,7},{7,5},{8,10},{10,8},{9,1... | collective-permute-start | bytes 1769480 | tf_op jit(solution)/shard_map/ppermute | solution.py:102
  68.7 22.1 %collective-permute-done.6 = bf16[2,384,256]{1,2,0:T(8,128)(2,1)S(1)} collective-permute-done((bf16[2,384,256]{1,2,0:T(8,128)(2,1)S(1)}, bf16[2,384,256]{1,2,0:T(8,128)(2,1)S(1)}, u32[]{:S(2)}, u32[]{:S(2)}) %collective-permute-start.6) | collective-permute-done | bytes 393248 | tf_op jit(solution)/shard_map/ppermute | solution.py:102
  91.5 1.5 %convolution_convert_fusion.4 = bf16[384,256]{0,1:T(8,128)(2,1)S(1)} fusion(bf16[384,768]{1,0:T(8,128)(2,1)S(1)} %get-tuple-element.16, f32[384]{0:T(512)S(1)} %add_rsqrt_fusion.1, f32[384]{0:T(512)S(1)} %broadcast_multiply_fusion.1, bf16[3,768,256]{2,1,0:T(8,128)(2,1)} %param.12), kind=kOutput, calls=%fused_computation.106 | convolution fusion | flops 152272896 | bytes 1182720 | tf_op jit(solution)/shard_map/dot_general | solution.py:36
  93.0 0.5 multiply_reduce_fusion.2
  93.6 0.5 multiply_reduce_fusion.1
  94.1 0.5 multiply_reduce_fusion
  96.9 0.5 fusion.30
  97.4 0.6 fusion.31
  98.0 0.5 fusion.32
  98.6 0.6 fusion.71
  99.9 1.6 %collective-permute-start.8 = (bf16[384,768]{1,0:T(8,128)(2,1)S(1)}, bf16[384,768]{1,0:T(8,128)(2,1)}, u32[]{:S(2)}, u32[]{:S(2)}) collective-permute-start(bf16[384,768]{1,0:T(8,128)(2,1)S(1)} %convolution_convert_fusion), channel_id=1, source_target_pairs={{0,2},{2,0},{1,3},{3,1},{4,6},{6,4},{5,7},{7,5},{8,10},{10,8},{9,1... | collective-permute-start | bytes 1769480 | tf_op jit(solution)/shard_map/ppermute | solution.py:102
  101.5 0.5 collective-permute-start.9
  102.0 17.3 %collective-permute-done.9 = bf16[384,256]{1,0:T(8,128)(2,1)S(1)} collective-permute-done((bf16[384,256]{1,0:T(8,128)(2,1)S(1)}, bf16[384,256]{1,0:T(8,128)(2,1)S(1)}, u32[]{:S(2)}, u32[]{:S(2)}) %collective-permute-start.9) | collective-permute-done | bytes 196640 | tf_op jit(solution)/shard_map/ppermute | solution.py:102
  119.4 0.6 gather_fusion.1
  120.1 1.3 fusion.41
  121.9 13.1 %collective-permute-start.10 = (bf16[1,66,256]{2,1,0:T(8,128)(2,1)S(1)}, bf16[1,66,256]{2,1,0:T(8,128)(2,1)S(1)}, u32[]{:S(2)}, u32[]{:S(2)}) collective-permute-start(bf16[1,66,256]{2,1,0:T(8,128)(2,1)S(1)} %get-tuple-element.38), channel_id=1, source_target_pairs={{0,4},{4,8},{8,12},{1,5},{5,9},{9,13},{2,6},{6,10},{10,14},{3,7},{... | collective-permute-start | bytes 101384 | tf_op jit(solution)/shard_map/ppermute | solution.py:19
  135.0 1.3 collective-permute-start.11
  136.8 4.1 %collective-permute-done.11 = bf16[1,66,256]{2,1,0:T(8,128)(2,1)S(1)} collective-permute-done((bf16[1,66,256]{2,1,0:T(8,128)(2,1)S(1)}, bf16[1,66,256]{2,1,0:T(8,128)(2,1)S(1)}, u32[]{:S(2)}, u32[]{:S(2)}) %collective-permute-start.11) | collective-permute-done | bytes 33824 | tf_op jit(solution)/shard_map/ppermute | solution.py:21
  140.9 1.1 fusion.78
  (80 shorter events, 10.4 us)
Async XLA Ops:
  0.0 140.9 %copy-start = (bf16[3,3,256,256]{3,2,1,0:T(8,128)(2,1)S(1)}, bf16[3,3,256,256]{3,2,1,0:T(8,128)(2,1)}, u32[]{:S(2)}) copy-start(bf16[3,3,256,256]{3,2,1,0:T(8,128)(2,1)} %param.15) | copy-start | bytes 3538948
  2.1 16.4 %collective-permute-start = (bf16[2,384,384]{2,1,0:T(8,128)(2,1)S(1)}, bf16[2,384,384]{2,1,0:T(8,128)(2,1)S(1)}, u32[]{:S(2)}, u32[]{:S(2)}) collective-permute-start(bf16[2,384,384]{2,1,0:T(8,128)(2,1)S(1)} %constant_dynamic-update-slice_fusion), channel_id=1, source_target_pairs={{0,2},{2,0},{1,3},{3,1},{4,6},{6,4},{5,7},{7,5},{8,10},{10,8},{9,1... | collective-permute-start | bytes 1769480 | tf_op jit(solution)/shard_map/ppermute | solution.py:102
  23.3 8.9 %copy-start.4 = (bf16[384,256]{0,1:T(8,128)(2,1)}, bf16[384,256]{0,1:T(8,128)(2,1)S(1)}, u32[]{:S(2)}) copy-start(bf16[384,256]{0,1:T(8,128)(2,1)S(1)} %convolution_convert_fusion.6) | copy-start | bytes 589828
  24.8 7.4 %copy-start.2 = (bf16[384,256]{0,1:T(8,128)(2,1)}, bf16[384,256]{0,1:T(8,128)(2,1)S(1)}, u32[]{:S(2)}) copy-start(bf16[384,256]{0,1:T(8,128)(2,1)S(1)} %convolution_convert_fusion.5) | copy-start | bytes 589828
  27.7 14.3 %collective-permute-start.1 = (bf16[2,384,256]{1,2,0:T(8,128)(2,1)}, bf16[2,384,256]{1,2,0:T(8,128)(2,1)}, u32[]{:S(2)}, u32[]{:S(2)}) collective-permute-start(bf16[2,384,256]{1,2,0:T(8,128)(2,1)} %pad_maximum_fusion.1), channel_id=1, source_target_pairs={{0,4},{4,8},{8,12},{12,0},{1,5},{5,9},{9,13},{13,1},{2,6},{6,10},{... | collective-permute-start | bytes 1179656 | tf_op jit(solution)/shard_map/ppermute | solution.py:102
  29.6 29.4 %collective-permute-start.2 = (bf16[2,384,256]{1,2,0:T(8,128)(2,1)}, bf16[2,384,256]{1,2,0:T(8,128)(2,1)}, u32[]{:S(2)}, u32[]{:S(2)}) collective-permute-start(bf16[2,384,256]{1,2,0:T(8,128)(2,1)} %pad_maximum_fusion.1), channel_id=1, source_target_pairs={{0,8},{4,12},{8,0},{12,4},{1,9},{5,13},{9,1},{13,5},{2,10},{6,14},... | collective-permute-start | bytes 1179656 | tf_op jit(solution)/shard_map/ppermute | solution.py:102
  32.1 28.4 %collective-permute-start.3 = (bf16[2,384,256]{1,2,0:T(8,128)(2,1)}, bf16[2,384,256]{1,2,0:T(8,128)(2,1)}, u32[]{:S(2)}, u32[]{:S(2)}) collective-permute-start(bf16[2,384,256]{1,2,0:T(8,128)(2,1)} %pad_maximum_fusion.1), channel_id=1, source_target_pairs={{0,12},{4,0},{8,4},{12,8},{1,13},{5,1},{9,5},{13,9},{2,14},{6,2},{... | collective-permute-start | bytes 1179656 | tf_op jit(solution)/shard_map/ppermute | solution.py:102
  36.4 2.7 %copy-start.1 = (bf16[384,256]{0,1:T(8,128)(2,1)S(1)}, bf16[384,256]{0,1:T(8,128)(2,1)}, u32[]{:S(2)}) copy-start(bf16[384,256]{0,1:T(8,128)(2,1)} %convolution_convert_fusion.7) | copy-start | bytes 589828
  36.4 2.7 %copy-start.5 = (bf16[384,256]{0,1:T(8,128)(2,1)S(1)}, bf16[384,256]{0,1:T(8,128)(2,1)}, u32[]{:S(2)}) copy-start(bf16[384,256]{0,1:T(8,128)(2,1)} %copy-done.4) | copy-start | bytes 589828
  37.9 30.7 %collective-permute-start.5 = (bf16[2,384,256]{1,2,0:T(8,128)(2,1)S(1)}, bf16[2,384,256]{1,2,0:T(8,128)(2,1)S(1)}, u32[]{:S(2)}, u32[]{:S(2)}) collective-permute-start(bf16[2,384,256]{1,2,0:T(8,128)(2,1)S(1)} %pad_maximum_fusion.2), channel_id=1, source_target_pairs={{0,4},{4,8},{8,12},{12,0},{1,5},{5,9},{9,13},{13,1},{2,6},{6,10},{... | collective-permute-start | bytes 1179656 | tf_op jit(solution)/shard_map/ppermute | solution.py:102
  38.7 52.1 %collective-permute-start.6 = (bf16[2,384,256]{1,2,0:T(8,128)(2,1)S(1)}, bf16[2,384,256]{1,2,0:T(8,128)(2,1)S(1)}, u32[]{:S(2)}, u32[]{:S(2)}) collective-permute-start(bf16[2,384,256]{1,2,0:T(8,128)(2,1)S(1)} %pad_maximum_fusion.2), channel_id=1, source_target_pairs={{0,8},{4,12},{8,0},{12,4},{1,9},{5,13},{9,1},{13,5},{2,10},{6,14},... | collective-permute-start | bytes 1179656 | tf_op jit(solution)/shard_map/ppermute | solution.py:102
  42.0 48.8 %collective-permute-start.7 = (bf16[2,384,256]{1,2,0:T(8,128)(2,1)S(1)}, bf16[2,384,256]{1,2,0:T(8,128)(2,1)S(1)}, u32[]{:S(2)}, u32[]{:S(2)}) collective-permute-start(bf16[2,384,256]{1,2,0:T(8,128)(2,1)S(1)} %pad_maximum_fusion.2), channel_id=1, source_target_pairs={{0,12},{4,0},{8,4},{12,8},{1,13},{5,1},{9,5},{13,9},{2,14},{6,2},{... | collective-permute-start | bytes 1179656 | tf_op jit(solution)/shard_map/ppermute | solution.py:102
  62.9 0.9 copy-start.3
  65.5 1.0 copy-start.6
  66.9 24.0 %collective-permute-start.4 = (bf16[384,768]{1,0:T(8,128)(2,1)S(1)}, bf16[384,768]{1,0:T(8,128)(2,1)S(1)}, u32[]{:S(2)}, u32[]{:S(2)}) collective-permute-start(bf16[384,768]{1,0:T(8,128)(2,1)S(1)} %convolution_convert_fusion.1), channel_id=1, source_target_pairs={{0,2},{2,0},{1,3},{3,1},{4,6},{6,4},{5,7},{7,5},{8,10},{10,8},{9,1... | collective-permute-start | bytes 1769480 | tf_op jit(solution)/shard_map/ppermute | solution.py:102
  98.5 1.0 copy-start.7
  98.6 2.9 %copy-start.8 = (bf16[384,256]{1,0:T(8,128)(2,1)S(1)}, bf16[384,256]{1,0:T(8,128)(2,1)}, u32[]{:S(2)}) copy-start(bf16[384,256]{1,0:T(8,128)(2,1)} %param.14) | copy-start | bytes 589828
  99.9 20.2 %collective-permute-start.8 = (bf16[384,768]{1,0:T(8,128)(2,1)S(1)}, bf16[384,768]{1,0:T(8,128)(2,1)}, u32[]{:S(2)}, u32[]{:S(2)}) collective-permute-start(bf16[384,768]{1,0:T(8,128)(2,1)S(1)} %convolution_convert_fusion), channel_id=1, source_target_pairs={{0,2},{2,0},{1,3},{3,1},{4,6},{6,4},{5,7},{7,5},{8,10},{10,8},{9,1... | collective-permute-start | bytes 1769480 | tf_op jit(solution)/shard_map/ppermute | solution.py:102
  101.5 17.9 %collective-permute-start.9 = (bf16[384,256]{1,0:T(8,128)(2,1)S(1)}, bf16[384,256]{1,0:T(8,128)(2,1)S(1)}, u32[]{:S(2)}, u32[]{:S(2)}) collective-permute-start(bf16[384,256]{1,0:T(8,128)(2,1)S(1)} %copy-done.8), channel_id=1, source_target_pairs={{0,2},{2,0},{1,3},{3,1},{4,6},{6,4},{5,7},{7,5},{8,10},{10,8},{9,1... | collective-permute-start | bytes 589832 | tf_op jit(solution)/shard_map/ppermute | solution.py:102
  121.9 14.7 %collective-permute-start.10 = (bf16[1,66,256]{2,1,0:T(8,128)(2,1)S(1)}, bf16[1,66,256]{2,1,0:T(8,128)(2,1)S(1)}, u32[]{:S(2)}, u32[]{:S(2)}) collective-permute-start(bf16[1,66,256]{2,1,0:T(8,128)(2,1)S(1)} %get-tuple-element.38), channel_id=1, source_target_pairs={{0,4},{4,8},{8,12},{1,5},{5,9},{9,13},{2,6},{6,10},{10,14},{3,7},{... | collective-permute-start | bytes 101384 | tf_op jit(solution)/shard_map/ppermute | solution.py:19
  135.0 5.9 %collective-permute-start.11 = (bf16[1,66,256]{2,1,0:T(8,128)(2,1)S(1)}, bf16[1,66,256]{2,1,0:T(8,128)(2,1)S(1)}, u32[]{:S(2)}, u32[]{:S(2)}) collective-permute-start(bf16[1,66,256]{2,1,0:T(8,128)(2,1)S(1)} %get-tuple-element.37), channel_id=1, source_target_pairs={{4,0},{8,4},{12,8},{5,1},{9,5},{13,9},{6,2},{10,6},{14,10},{7,3},{... | collective-permute-start | bytes 101384 | tf_op jit(solution)/shard_map/ppermute | solution.py:21

commit v4 on v3

--- a/solution.py
+++ b/solution.py
@@ -124,10 +124,9 @@
     tiles = lax.axis_size("tile")
     tile_index = lax.axis_index("tile")
     token_count, feature_share = left_tokens.shape[1], left_tokens.shape[2]
-    tokens = gather_ordered(jnp.stack([left_tokens[0], right_tokens[0]]), "tile")
     left_full, right_full = (
-        jnp.moveaxis(tokens[:, side], 0, 1).reshape(token_count, tiles * feature_share)
-        for side in range(2)
+        jnp.moveaxis(gather_ordered(side[0], "tile"), 0, 1).reshape(token_count, tiles * feature_share)
+        for side in (left_tokens, right_tokens)
     )
     reassemble_full = gather_ordered(reassemble, "tile").reshape(-1, CH)
     left_normed = layer_norm(left_full)

time: 143 us -> 138 us (0.965)
  waiting for transfers between devices: 71.9 us -> 33.4 us
  starting transfers between devices: 31 us -> 64.4 us
  other arithmetic: 8.64 us -> 11.7 us
  local copies, waits for them, and re-layouts: 9.78 us -> 8.16 us
    ppermute x10 -> x11, waiting for transfers between devices: 67.5 us -> 29 us  [shifted(): lax.ppermute(value, axis, [(i, (i + shift) % count) for i in range(count)])]
    ppermute x10 -> x11, starting transfers between devices: 16.6 us -> 53 us  [shifted(): lax.ppermute(value, axis, [(i, (i + shift) % count) for i in range(count)])]
    ppermute x1, starting transfers between devices: 13.1 us -> 10.1 us  [padded_2(): lax.ppermute(tail, axis, [(i, (i + 1) % count) for i in range(ends)])]
    another operation x2 -> x3, other arithmetic: 0.17 us -> 3.02 us  [gather_ordered(): stack = jnp.stack(shifted(value, axis))]
  transfers between devices with their start and end apart: 12 -> 13, of which waited for: 7 -> 8; matrix products, arithmetic and copies ran while one was open for 11% -> 26% of each run, Pallas kernels for 0% -> 0%
where the time goes in v4:
time: 138 us; the launch traced here: 137 us
  starting transfers between devices  64.4 us (47%)
  waiting for transfers between devices  33.4 us (24%)
  matrix products  19.3 us (14%)
  other arithmetic  11.7 us (8%)
  local copies, waits for them, and re-layouts  8.16 us (6%)
    ppermute x11, starting transfers between devices, shifted(): lax.ppermute(value, axis, [(i, (i + shift) % count) for i in range(count)])  53 us
    ppermute x11, waiting for transfers between devices, shifted(): lax.ppermute(value, axis, [(i, (i + shift) % count) for i in range(count)])  29 us
    ppermute x1, starting transfers between devices, padded_2(): lax.ppermute(tail, axis, [(i, (i + 1) % count) for i in range(ends)])  10.1 us
    dot_general x6, matrix products, project_rows(): jnp.dot(normed, weight, preferred_element_type=jnp.float32)  8.62 us
    dot_general x8, matrix products, attend_keys(): jnp.einsum('hqk,khd->qhd', expanded.astype(jnp.bfloat16), values_rows.res...  4.4 us
    dot_general x8, matrix products, attend_keys(): jnp.einsum('qhd,khd->hqk', queries.reshape(query_count, head_count, HD),...  4.25 us
    ppermute x1, waiting for transfers between devices, padded_2(): lax.ppermute(head, axis, [((i + 1) % count, i) for i in range(ends)])  4.07 us
    reduce_sum x8, other arithmetic, attend_keys(): totals = totals * correction + jnp.sum(expanded, axis=2)  3.23 us
  transfers between devices with their start and end apart: 13, of which 8 were waited for; matrix products, arithmetic and copies ran while one was open for 26% of the time, Pallas kernels for 0%

profile of v4, /device:TPU:0, one launch (start us, length us, event | category | flops | bytes accessed | tf_op | source)
XLA Modules:
  0.0 137.5 jit_solution(9809743477718292415)
XLA Ops:
  0.0 3.0 %collective-permute-start = (bf16[384,384]{1,0:T(8,128)(2,1)}, bf16[384,384]{1,0:T(8,128)(2,1)S(1)}, u32[]{:S(2)}, u32[]{:S(2)}) collective-permute-start(bf16[384,384]{1,0:T(8,128)(2,1)} %bitcast.321), channel_id=1, source_target_pairs={{0,2},{2,0},{1,3},{3,1},{4,6},{6,4},{5,7},{7,5},{8,10},{10,8},{9,1... | collective-permute-start | bytes 884744 | tf_op jit(solution)/shard_map/ppermute | solution.py:102
  3.0 2.0 %collective-permute-start.10 = (bf16[384,256]{1,0:T(8,128)(2,1)}, bf16[384,256]{1,0:T(8,128)(2,1)}, u32[]{:S(2)}, u32[]{:S(2)}) collective-permute-start(bf16[384,256]{1,0:T(8,128)(2,1)} %param.16), channel_id=1, source_target_pairs={{0,2},{2,0},{1,3},{3,1},{4,6},{6,4},{5,7},{7,5},{8,10},{10,8},{9,1... | collective-permute-start | bytes 589832 | tf_op jit(solution)/shard_map/ppermute | solution.py:102
  5.0 6.0 %collective-permute-done = bf16[384,384]{1,0:T(8,128)(2,1)S(1)} collective-permute-done((bf16[384,384]{1,0:T(8,128)(2,1)}, bf16[384,384]{1,0:T(8,128)(2,1)S(1)}, u32[]{:S(2)}, u32[]{:S(2)}) %collective-permute-start) | collective-permute-done | bytes 294944 | tf_op jit(solution)/shard_map/ppermute | solution.py:102
  11.0 1.0 pad_maximum_fusion
  12.1 5.3 %collective-permute-done.5 = bf16[384,384]{1,0:T(8,128)(2,1)S(1)} collective-permute-done((bf16[384,384]{1,0:T(8,128)(2,1)}, bf16[384,384]{1,0:T(8,128)(2,1)S(1)}, u32[]{:S(2)}, u32[]{:S(2)}) %collective-permute-start.5) | collective-permute-done | bytes 294944 | tf_op jit(solution)/shard_map/ppermute | solution.py:102
  17.4 1.0 pad_maximum_fusion.1
  18.4 0.7 gather_fusion.1
  19.1 0.7 gather_fusion.2
  20.1 0.6 fusion.42
  20.7 1.2 fusion.77
  22.3 1.4 %convolution_convert_fusion.6 = bf16[384,256]{0,1:T(8,128)(2,1)S(1)} fusion(bf16[384,768]{0,1:T(8,128)(2,1)S(1)} %bitcast.316, bf16[3,768,256]{2,1,0:T(8,128)(2,1)} %param.12), kind=kOutput, calls=%fused_computation.105 | convolution fusion | flops 151093248 | bytes 1179648 | tf_op jit(solution)/shard_map/dot_general | solution.py:36
  23.7 1.4 %convolution_convert_fusion.5 = bf16[384,256]{0,1:T(8,128)(2,1)S(1)} fusion(bf16[384,768]{0,1:T(8,128)(2,1)S(1)} %bitcast.317, bf16[3,768,256]{2,1,0:T(8,128)(2,1)} %param.12), kind=kOutput, calls=%fused_computation.104 | convolution fusion | flops 151093248 | bytes 1179648 | tf_op jit(solution)/shard_map/dot_general | solution.py:36
  25.1 1.4 %convolution_convert_fusion.7 = bf16[384,256]{0,1:T(8,128)(2,1)S(1)} fusion(bf16[384,768]{0,1:T(8,128)(2,1)S(1)} %bitcast.318, bf16[3,768,256]{2,1,0:T(8,128)(2,1)} %param.12), kind=kOutput, calls=%fused_computation.106 | convolution fusion | flops 151093248 | bytes 1179648 | tf_op jit(solution)/shard_map/dot_general | solution.py:36
  26.5 0.8 pad_maximum_fusion.2
  27.3 2.1 %collective-permute-start.1 = (bf16[2,384,256]{1,2,0:T(8,128)(2,1)}, bf16[2,384,256]{1,2,0:T(8,128)(2,1)}, u32[]{:S(2)}, u32[]{:S(2)}) collective-permute-start(bf16[2,384,256]{1,2,0:T(8,128)(2,1)} %pad_maximum_fusion.2), channel_id=1, source_target_pairs={{0,4},{4,8},{8,12},{12,0},{1,5},{5,9},{9,13},{13,1},{2,6},{6,10},{... | collective-permute-start | bytes 1179656 | tf_op jit(solution)/shard_map/ppermute | solution.py:102
  29.4 2.6 %collective-permute-start.2 = (bf16[2,384,256]{1,2,0:T(8,128)(2,1)}, bf16[2,384,256]{1,2,0:T(8,128)(2,1)}, u32[]{:S(2)}, u32[]{:S(2)}) collective-permute-start(bf16[2,384,256]{1,2,0:T(8,128)(2,1)} %pad_maximum_fusion.2), channel_id=1, source_target_pairs={{0,8},{4,12},{8,0},{12,4},{1,9},{5,13},{9,1},{13,5},{2,10},{6,14},... | collective-permute-start | bytes 1179656 | tf_op jit(solution)/shard_map/ppermute | solution.py:102
  32.0 1.3 collective-permute-start.3
  33.5 1.4 copy.33
  34.9 1.4 %convolution_convert_fusion.3 = bf16[384,256]{0,1:T(8,128)(2,1)S(1)} fusion(bf16[384,768]{0,1:T(8,128)(2,1)S(1)} %bitcast.319, bf16[3,768,256]{2,1,0:T(8,128)(2,1)} %param.14), kind=kOutput, calls=%fused_computation.102 | convolution fusion | flops 151093248 | bytes 1179648 | tf_op jit(solution)/shard_map/dot_general | solution.py:36
  36.3 1.4 %convolution_convert_fusion.2 = bf16[384,256]{0,1:T(8,128)(2,1)S(1)} fusion(bf16[384,768]{0,1:T(8,128)(2,1)S(1)} %bitcast.320, bf16[3,768,256]{2,1,0:T(8,128)(2,1)} %param.14), kind=kOutput, calls=%fused_computation.101 | convolution fusion | flops 151093248 | bytes 1179648 | tf_op jit(solution)/shard_map/dot_general | solution.py:36
  37.9 0.7 collective-permute-start.6
  39.2 2.7 %collective-permute-done.1 = bf16[2,384,256]{1,2,0:T(8,128)(2,1)} collective-permute-done((bf16[2,384,256]{1,2,0:T(8,128)(2,1)}, bf16[2,384,256]{1,2,0:T(8,128)(2,1)}, u32[]{:S(2)}, u32[]{:S(2)}) %collective-permute-start.1) | collective-permute-done | bytes 393248 | tf_op jit(solution)/shard_map/ppermute | solution.py:102
  41.9 17.8 %collective-permute-start.7 = (bf16[2,384,256]{1,2,0:T(8,128)(2,1)S(1)}, bf16[2,384,256]{1,2,0:T(8,128)(2,1)S(1)}, u32[]{:S(2)}, u32[]{:S(2)}) collective-permute-start(bf16[2,384,256]{1,2,0:T(8,128)(2,1)S(1)} %pad_maximum_fusion.3), channel_id=1, source_target_pairs={{0,8},{4,12},{8,0},{12,4},{1,9},{5,13},{9,1},{13,5},{2,10},{6,14},... | collective-permute-start | bytes 1179656 | tf_op jit(solution)/shard_map/ppermute | solution.py:102
  59.7 1.1 fusion.142
  61.3 20.4 %collective-permute-start.8 = (bf16[2,384,256]{1,2,0:T(8,128)(2,1)S(1)}, bf16[2,384,256]{1,2,0:T(8,128)(2,1)S(1)}, u32[]{:S(2)}, u32[]{:S(2)}) collective-permute-start(bf16[2,384,256]{1,2,0:T(8,128)(2,1)S(1)} %pad_maximum_fusion.3), channel_id=1, source_target_pairs={{0,12},{4,0},{8,4},{12,8},{1,13},{5,1},{9,5},{13,9},{2,14},{6,2},{... | collective-permute-start | bytes 1179656 | tf_op jit(solution)/shard_map/ppermute | solution.py:102
  81.6 1.1 fusion.141
  83.2 1.1 fusion.140
  86.5 0.6 fusion.30
  87.1 0.5 fusion.31
  87.6 0.6 fusion.32
  88.2 0.6 fusion.72
  89.5 1.6 %collective-permute-start.4 = (bf16[384,768]{1,0:T(8,128)(2,1)S(1)}, bf16[384,768]{1,0:T(8,128)(2,1)S(1)}, u32[]{:S(2)}, u32[]{:S(2)}) collective-permute-start(bf16[384,768]{1,0:T(8,128)(2,1)S(1)} %convolution_convert_fusion.1), channel_id=1, source_target_pairs={{0,2},{2,0},{1,3},{3,1},{4,6},{6,4},{5,7},{7,5},{8,10},{10,8},{9,1... | collective-permute-start | bytes 1769480 | tf_op jit(solution)/shard_map/ppermute | solution.py:102
  91.2 1.8 %collective-permute-done.8 = bf16[2,384,256]{1,2,0:T(8,128)(2,1)S(1)} collective-permute-done((bf16[2,384,256]{1,2,0:T(8,128)(2,1)S(1)}, bf16[2,384,256]{1,2,0:T(8,128)(2,1)S(1)}, u32[]{:S(2)}, u32[]{:S(2)}) %collective-permute-start.8) | collective-permute-done | bytes 393248 | tf_op jit(solution)/shard_map/ppermute | solution.py:102
  93.0 6.5 %collective-permute-done.4 = bf16[384,768]{1,0:T(8,128)(2,1)S(1)} collective-permute-done((bf16[384,768]{1,0:T(8,128)(2,1)S(1)}, bf16[384,768]{1,0:T(8,128)(2,1)S(1)}, u32[]{:S(2)}, u32[]{:S(2)}) %collective-permute-start.4) | collective-permute-done | bytes 589856 | tf_op jit(solution)/shard_map/ppermute | solution.py:102
  100.1 1.5 %convolution_convert_fusion.4 = bf16[384,256]{0,1:T(8,128)(2,1)S(1)} fusion(bf16[384,768]{1,0:T(8,128)(2,1)S(1)} %get-tuple-element.17, f32[384]{0:T(512)S(1)} %add_rsqrt_fusion.1, f32[384]{0:T(512)S(1)} %broadcast_multiply_fusion.1, bf16[3,768,256]{2,1,0:T(8,128)(2,1)} %param.14), kind=kOutput, calls=%fused_computation.103 | convolution fusion | flops 152272896 | bytes 1182720 | tf_op jit(solution)/shard_map/dot_general | solution.py:36
  105.5 0.6 fusion.34
  106.0 0.5 fusion.35
  106.6 0.5 fusion.36
  107.2 0.5 fusion.69
  108.5 1.6 %collective-permute-start.9 = (bf16[384,768]{1,0:T(8,128)(2,1)S(1)}, bf16[384,768]{1,0:T(8,128)(2,1)}, u32[]{:S(2)}, u32[]{:S(2)}) collective-permute-start(bf16[384,768]{1,0:T(8,128)(2,1)S(1)} %convolution_convert_fusion), channel_id=1, source_target_pairs={{0,2},{2,0},{1,3},{3,1},{4,6},{6,4},{5,7},{7,5},{8,10},{10,8},{9,1... | collective-permute-start | bytes 1769480 | tf_op jit(solution)/shard_map/ppermute | solution.py:102
  110.1 1.0 pad_maximum_fusion.4
  111.1 0.6 gather_fusion
  111.8 6.8 %collective-permute-done.9 = bf16[384,768]{1,0:T(8,128)(2,1)} collective-permute-done((bf16[384,768]{1,0:T(8,128)(2,1)S(1)}, bf16[384,768]{1,0:T(8,128)(2,1)}, u32[]{:S(2)}, u32[]{:S(2)}) %collective-permute-start.9) | collective-permute-done | bytes 589856 | tf_op jit(solution)/shard_map/ppermute | solution.py:102
  118.5 1.3 fusion.44
  120.4 10.1 %collective-permute-start.11 = (bf16[1,66,256]{2,1,0:T(8,128)(2,1)S(1)}, bf16[1,66,256]{2,1,0:T(8,128)(2,1)S(1)}, u32[]{:S(2)}, u32[]{:S(2)}) collective-permute-start(bf16[1,66,256]{2,1,0:T(8,128)(2,1)S(1)} %get-tuple-element.37), channel_id=1, source_target_pairs={{0,4},{4,8},{8,12},{1,5},{5,9},{9,13},{2,6},{6,10},{10,14},{3,7},{... | collective-permute-start | bytes 101384 | tf_op jit(solution)/shard_map/ppermute | solution.py:19
  130.5 1.3 collective-permute-start.12
  132.2 4.1 %collective-permute-done.12 = bf16[1,66,256]{2,1,0:T(8,128)(2,1)S(1)} collective-permute-done((bf16[1,66,256]{2,1,0:T(8,128)(2,1)S(1)}, bf16[1,66,256]{2,1,0:T(8,128)(2,1)S(1)}, u32[]{:S(2)}, u32[]{:S(2)}) %collective-permute-start.12) | collective-permute-done | bytes 33824 | tf_op jit(solution)/shard_map/ppermute | solution.py:21
  136.4 1.1 fusion.76
  (73 shorter events, 12.1 us)
Async XLA Ops:
  0.0 136.4 %copy-start = (bf16[3,3,256,256]{3,2,1,0:T(8,128)(2,1)S(1)}, bf16[3,3,256,256]{3,2,1,0:T(8,128)(2,1)}, u32[]{:S(2)}) copy-start(bf16[3,3,256,256]{3,2,1,0:T(8,128)(2,1)} %param.17) | copy-start | bytes 3538948
  0.0 11.0 %collective-permute-start = (bf16[384,384]{1,0:T(8,128)(2,1)}, bf16[384,384]{1,0:T(8,128)(2,1)S(1)}, u32[]{:S(2)}, u32[]{:S(2)}) collective-permute-start(bf16[384,384]{1,0:T(8,128)(2,1)} %bitcast.321), channel_id=1, source_target_pairs={{0,2},{2,0},{1,3},{3,1},{4,6},{6,4},{5,7},{7,5},{8,10},{10,8},{9,1... | collective-permute-start | bytes 884744 | tf_op jit(solution)/shard_map/ppermute | solution.py:102
  3.0 14.4 %collective-permute-start.5 = (bf16[384,384]{1,0:T(8,128)(2,1)}, bf16[384,384]{1,0:T(8,128)(2,1)S(1)}, u32[]{:S(2)}, u32[]{:S(2)}) collective-permute-start(bf16[384,384]{1,0:T(8,128)(2,1)} %bitcast.322), channel_id=1, source_target_pairs={{0,2},{2,0},{1,3},{3,1},{4,6},{6,4},{5,7},{7,5},{8,10},{10,8},{9,1... | collective-permute-start | bytes 884744 | tf_op jit(solution)/shard_map/ppermute | solution.py:102
  3.0 107.0 %collective-permute-start.10 = (bf16[384,256]{1,0:T(8,128)(2,1)}, bf16[384,256]{1,0:T(8,128)(2,1)}, u32[]{:S(2)}, u32[]{:S(2)}) collective-permute-start(bf16[384,256]{1,0:T(8,128)(2,1)} %param.16), channel_id=1, source_target_pairs={{0,2},{2,0},{1,3},{3,1},{4,6},{6,4},{5,7},{7,5},{8,10},{10,8},{9,1... | collective-permute-start | bytes 589832 | tf_op jit(solution)/shard_map/ppermute | solution.py:102
  27.3 14.5 %collective-permute-start.1 = (bf16[2,384,256]{1,2,0:T(8,128)(2,1)}, bf16[2,384,256]{1,2,0:T(8,128)(2,1)}, u32[]{:S(2)}, u32[]{:S(2)}) collective-permute-start(bf16[2,384,256]{1,2,0:T(8,128)(2,1)} %pad_maximum_fusion.2), channel_id=1, source_target_pairs={{0,4},{4,8},{8,12},{12,0},{1,5},{5,9},{9,13},{13,1},{2,6},{6,10},{... | collective-permute-start | bytes 1179656 | tf_op jit(solution)/shard_map/ppermute | solution.py:102
  29.4 31.8 %collective-permute-start.2 = (bf16[2,384,256]{1,2,0:T(8,128)(2,1)}, bf16[2,384,256]{1,2,0:T(8,128)(2,1)}, u32[]{:S(2)}, u32[]{:S(2)}) collective-permute-start(bf16[2,384,256]{1,2,0:T(8,128)(2,1)} %pad_maximum_fusion.2), channel_id=1, source_target_pairs={{0,8},{4,12},{8,0},{12,4},{1,9},{5,13},{9,1},{13,5},{2,10},{6,14},... | collective-permute-start | bytes 1179656 | tf_op jit(solution)/shard_map/ppermute | solution.py:102
  32.0 51.2 %collective-permute-start.3 = (bf16[2,384,256]{1,2,0:T(8,128)(2,1)}, bf16[2,384,256]{1,2,0:T(8,128)(2,1)}, u32[]{:S(2)}, u32[]{:S(2)}) collective-permute-start(bf16[2,384,256]{1,2,0:T(8,128)(2,1)} %pad_maximum_fusion.2), channel_id=1, source_target_pairs={{0,12},{4,0},{8,4},{12,8},{1,13},{5,1},{9,5},{13,9},{2,14},{6,2},{... | collective-permute-start | bytes 1179656 | tf_op jit(solution)/shard_map/ppermute | solution.py:102
  37.9 53.2 %collective-permute-start.6 = (bf16[2,384,256]{1,2,0:T(8,128)(2,1)S(1)}, bf16[2,384,256]{1,2,0:T(8,128)(2,1)S(1)}, u32[]{:S(2)}, u32[]{:S(2)}) collective-permute-start(bf16[2,384,256]{1,2,0:T(8,128)(2,1)S(1)} %pad_maximum_fusion.3), channel_id=1, source_target_pairs={{0,4},{4,8},{8,12},{12,0},{1,5},{5,9},{9,13},{13,1},{2,6},{6,10},{... | collective-permute-start | bytes 1179656 | tf_op jit(solution)/shard_map/ppermute | solution.py:102
  41.9 49.3 %collective-permute-start.7 = (bf16[2,384,256]{1,2,0:T(8,128)(2,1)S(1)}, bf16[2,384,256]{1,2,0:T(8,128)(2,1)S(1)}, u32[]{:S(2)}, u32[]{:S(2)}) collective-permute-start(bf16[2,384,256]{1,2,0:T(8,128)(2,1)S(1)} %pad_maximum_fusion.3), channel_id=1, source_target_pairs={{0,8},{4,12},{8,0},{12,4},{1,9},{5,13},{9,1},{13,5},{2,10},{6,14},... | collective-permute-start | bytes 1179656 | tf_op jit(solution)/shard_map/ppermute | solution.py:102
  61.3 31.7 %collective-permute-start.8 = (bf16[2,384,256]{1,2,0:T(8,128)(2,1)S(1)}, bf16[2,384,256]{1,2,0:T(8,128)(2,1)S(1)}, u32[]{:S(2)}, u32[]{:S(2)}) collective-permute-start(bf16[2,384,256]{1,2,0:T(8,128)(2,1)S(1)} %pad_maximum_fusion.3), channel_id=1, source_target_pairs={{0,12},{4,0},{8,4},{12,8},{1,13},{5,1},{9,5},{13,9},{2,14},{6,2},{... | collective-permute-start | bytes 1179656 | tf_op jit(solution)/shard_map/ppermute | solution.py:102
  88.2 1.0 copy-start.1
  89.5 9.9 %collective-permute-start.4 = (bf16[384,768]{1,0:T(8,128)(2,1)S(1)}, bf16[384,768]{1,0:T(8,128)(2,1)S(1)}, u32[]{:S(2)}, u32[]{:S(2)}) collective-permute-start(bf16[384,768]{1,0:T(8,128)(2,1)S(1)} %convolution_convert_fusion.1), channel_id=1, source_target_pairs={{0,2},{2,0},{1,3},{3,1},{4,6},{6,4},{5,7},{7,5},{8,10},{10,8},{9,1... | collective-permute-start | bytes 1769480 | tf_op jit(solution)/shard_map/ppermute | solution.py:102
  107.1 1.0 copy-start.2
  107.1 2.9 %copy-start.3 = (bf16[384,256]{1,0:T(8,128)(2,1)S(1)}, bf16[384,256]{1,0:T(8,128)(2,1)}, u32[]{:S(2)}) copy-start(bf16[384,256]{1,0:T(8,128)(2,1)} %param.16) | copy-start | bytes 589828
  108.5 10.1 %collective-permute-start.9 = (bf16[384,768]{1,0:T(8,128)(2,1)S(1)}, bf16[384,768]{1,0:T(8,128)(2,1)}, u32[]{:S(2)}, u32[]{:S(2)}) collective-permute-start(bf16[384,768]{1,0:T(8,128)(2,1)S(1)} %convolution_convert_fusion), channel_id=1, source_target_pairs={{0,2},{2,0},{1,3},{3,1},{4,6},{6,4},{5,7},{7,5},{8,10},{10,8},{9,1... | collective-permute-start | bytes 1769480 | tf_op jit(solution)/shard_map/ppermute | solution.py:102
  120.4 11.7 %collective-permute-start.11 = (bf16[1,66,256]{2,1,0:T(8,128)(2,1)S(1)}, bf16[1,66,256]{2,1,0:T(8,128)(2,1)S(1)}, u32[]{:S(2)}, u32[]{:S(2)}) collective-permute-start(bf16[1,66,256]{2,1,0:T(8,128)(2,1)S(1)} %get-tuple-element.37), channel_id=1, source_target_pairs={{0,4},{4,8},{8,12},{1,5},{5,9},{9,13},{2,6},{6,10},{10,14},{3,7},{... | collective-permute-start | bytes 101384 | tf_op jit(solution)/shard_map/ppermute | solution.py:19
  130.5 5.9 %collective-permute-start.12 = (bf16[1,66,256]{2,1,0:T(8,128)(2,1)S(1)}, bf16[1,66,256]{2,1,0:T(8,128)(2,1)S(1)}, u32[]{:S(2)}, u32[]{:S(2)}) collective-permute-start(bf16[1,66,256]{2,1,0:T(8,128)(2,1)S(1)} %get-tuple-element.36), channel_id=1, source_target_pairs={{4,0},{8,4},{12,8},{5,1},{9,5},{13,9},{6,2},{10,6},{14,10},{7,3},{... | collective-permute-start | bytes 101384 | tf_op jit(solution)/shard_map/ppermute | solution.py:21
